TPU v7x, 32 devices: a whole 2x2x4 slice. The times are simulated.
32 devices in a mesh: role: 2 (over y), tile: 16 (over z, x, core).
Axes of the slice: x: 2, y: 2, z: 4, core: 2. Of those that a mesh axis runs over, the one named last changes fastest.
Arguments:
- fields_pair: float32 [2, 512, 16384], P('role', None, 'tile'), may hold values from 0 to 1
- velocity: float32 [16384], P('tile'), may hold values from -0.5 to 0.5
- growth: float32 [16384], P('tile'), may hold values from 0.05 to 0.5
- features: bfloat16 [512, 1024], replicated, may hold values from -6 to 6
- assignment: int32 [512], replicated, may hold values from 0 to 511, each once
- out_pair: float32 [2, 1024, 16384], P('role', None, 'tile'), may hold values from -0.1875 to 0.1875
- hidden_pair: float32 [2, 5, 1024, 1024], P('role', None, 'tile'), may hold values from -0.1875 to 0.1875
Outputs:
- fields_next: float32 [2, 512, 16384], P('role', None, 'tile')
- out_next: float32 [2, 1024, 16384], P('role', None, 'tile')
- hidden_next: float32 [2, 5, 1024, 1024], P('role', None, 'tile')
Inputs may be any that keep to these rules, and one draw needn't show every extreme that they name: `assignment`: a permutation of the 512 members.
All inputs are finite; a program needn't handle non-finite values.
Results may differ from a plain program's by a relative error of at most 0.0022.
The roundings to bfloat16 on the way count: a program that leaves them out, or rounds other values in their place, can miss the bound.
Values may be sent and summed in bfloat16 or wider, within the bound.
A program may use at most 192 MiB of HBM per device.

v0:
```python
import functools

import jax
import jax.numpy as jnp
from jax import lax
from jax.experimental import pallas as pl
from jax.experimental.pallas import tpu as pltpu
from jax.sharding import PartitionSpec as P

momentum_decay = 0.9
step_size = 0.1


def extended(value, axis, dim, width):
    count, length = (lax.axis_size(axis), value.shape[dim])
    up = [(i, (i + 1) % count) for i in range(count)]
    down = [(j, i) for i, j in up]
    last = lax.slice_in_dim(value, length - width, length, axis=dim)
    leading = lax.slice_in_dim(value, 0, width, axis=dim)
    before = lax.ppermute(last, axis, up)
    after = lax.ppermute(leading, axis, down)
    return jnp.concatenate([before, value, after], axis=dim)


def silu_slope(values):
    logistic = jax.nn.sigmoid(values)
    return logistic * (1.0 + values * (1.0 - logistic))


def advance(padded, growth):
    states = padded[:-1]
    velocity_row = padded[-1]
    outflow = (
        jnp.maximum(velocity_row[:-1], 0.0) * states[:, :-1]
        + jnp.minimum(velocity_row[:-1], 0.0) * states[:, 1:]
    )
    carried = states[:, 1:-1] - outflow[:, 1:] + outflow[:, :-1]
    return carried + growth * carried * (1.0 - carried)


def to_trainer(value):
    return lax.ppermute(value.astype(jnp.bfloat16), "role", [(0, 1)])


def to_solver(value):
    return lax.ppermute(value.astype(jnp.bfloat16), "role", [(1, 0)])


def plain_training(features, hidden_narrow, out_narrow, own_fields, own_out, own_hidden, fields):
    layer_count, unit_rows = own_hidden.shape[:2]
    batch = own_fields.shape[0]
    first_unit = lax.axis_index("tile") * unit_rows
    momentum_out = to_trainer(own_out)
    momentum_hidden = to_trainer(own_hidden)
    full_hidden = [
        lax.all_gather(hidden_narrow[i], "tile", axis=0, tiled=True) for i in range(layer_count)
    ]
    inputs, summed_list = [], []
    activation = features
    for i in range(layer_count):
        inputs.append(activation)
        summed = jnp.dot(activation, full_hidden[i], preferred_element_type=jnp.float32)
        summed_list.append(summed)
        activation = jax.nn.silu(summed).astype(jnp.bfloat16)
    predicted = jnp.dot(activation, out_narrow, preferred_element_type=jnp.float32)
    residual = ((predicted - own_fields) / batch).astype(jnp.bfloat16)
    partial_grad = lax.dot_general(
        residual, out_narrow, (((1,), (1,)), ((), ())), preferred_element_type=jnp.float32
    )
    upstream = lax.psum(partial_grad, "tile")
    grad_out = jnp.dot(activation.T, residual, preferred_element_type=jnp.float32)
    sent_out = to_solver(grad_out)
    gradients, sent = [], []
    for i in reversed(range(layer_count)):
        slope = (upstream * silu_slope(summed_list[i])).astype(jnp.bfloat16)
        own_inputs = lax.dynamic_slice_in_dim(inputs[i], first_unit, unit_rows, 1)
        gradient = jnp.dot(own_inputs.T, slope, preferred_element_type=jnp.float32)
        gradients.append(gradient)
        sent.append(to_solver(gradient))
        if i > 0:
            upstream = lax.dot_general(
                slope, full_hidden[i], (((1,), (1,)), ((), ())), preferred_element_type=jnp.float32
            )
    solver_side = lax.axis_index("role") == 0
    grad_out = jnp.where(solver_side, sent_out.astype(jnp.float32), grad_out)
    other_hidden = jnp.where(solver_side, jnp.stack(sent[::-1]), momentum_hidden)
    return grad_out, jnp.stack(gradients[::-1]), momentum_out, other_hidden, to_trainer(fields)


LANES = 128
COLUMNS = 256


def train_kernel(
    groups,
    features_hbm,
    hidden_ref,
    out_hbm,
    target_hbm,
    fields_hbm,
    grad_out_ref,
    sent_hidden_ref,
    got_out_ref,
    got_hidden_ref,
    got_fields_ref,
    features_ref,
    out_ref,
    target_ref,
    weights,
    inputs,
    factors,
    residual,
    next_slope,
    got_residual,
    got_inputs,
    partial,
    slope,
    payload,
    payload_hidden,
    gradient,
    core_sum,
    x_away,
    x_sum,
    z_away,
    z_sum,
    z_send,
    z_recv,
    x_send,
    x_recv,
    core_send,
    core_recv,
    sum_send,
    sum_recv,
    slope_send,
    slope_recv,
    role_send,
    role_recv,
    local_sem,
):
    layer_count, unit_rows, width = hidden_ref.shape
    batch, cells = target_ref.shape
    rows = partial.shape[3]
    role = lax.axis_index("role")
    tile = lax.axis_index("tile")
    core = lax.rem(tile, 2)
    x = lax.rem(tile // 2, 2)
    z = tile // 4
    solver_side = role == 0

    def device(z_at, x_at, core_at):
        return (role, z_at * 4 + x_at * 2 + core_at)

    z_places = [lax.rem(z + k, groups) for k in range(1, groups)]
    z_origins = [lax.rem(z + groups - k, groups) for k in range(1, groups)]
    z_peers = [device(place, x, core) for place in z_places]
    x_peer = device(z, 1 - x, core)
    core_peer = device(z, x, 1 - core)
    role_peer = (1 - role, tile)
    sends = []

    def send(source, target, send_sem, recv_sem, peer):
        copy = pltpu.make_async_remote_copy(
            src_ref=source,
            dst_ref=target,
            send_sem=send_sem,
            recv_sem=recv_sem,
            device_id=peer,
            device_id_type=pl.DeviceIdType.MESH,
        )
        copy.start()
        sends.append(copy)
        return copy

    own = pltpu.make_async_copy(hidden_ref, weights.at[:, z, x, core], local_sem.at[0])
    own.start()
    loads = [
        pltpu.make_async_copy(features_hbm, features_ref, local_sem.at[1]),
        pltpu.make_async_copy(out_hbm, out_ref, local_sem.at[2]),
        pltpu.make_async_copy(target_hbm, target_ref, local_sem.at[3]),
    ]
    for load in loads:
        load.start()
    barrier = pltpu.get_barrier_semaphore()
    peers = z_peers + [x_peer, core_peer, role_peer]
    for peer in peers:
        pl.semaphore_signal(barrier, inc=1, device_id=peer, device_id_type=pl.DeviceIdType.MESH)
    pl.semaphore_wait(barrier, len(peers))

    x_copies = [[] for _ in range(layer_count)]

    def send_x(i, slot, source, place):
        x_copies[i].append(
            send(
                source,
                weights.at[i, place, x, core],
                x_send.at[i, slot],
                x_recv.at[i, slot],
                x_peer,
            )
        )

    z_copies = []
    for i in range(layer_count):
        z_copies.append(
            [
                send(
                    hidden_ref.at[i],
                    weights.at[i, z, x, core],
                    z_send.at[i, k],
                    z_recv.at[i, k],
                    z_peers[k],
                )
                for k in range(groups - 1)
            ]
        )
        if i < 3:
            send_x(i, 0, hidden_ref.at[i], z)
    last = layer_count - 1
    role_copies = []

    def send_role(source, target):
        slot = len(role_copies)
        copy = send(source, target, role_send.at[slot], role_recv.at[slot], role_peer)
        role_copies.append(copy)
        return copy

    send_role(fields_hbm, got_fields_ref)
    send_role(out_hbm, got_out_ref)
    own.wait()
    for load in loads:
        load.wait()

    def columns_of(j):
        return pl.ds(pl.multiple_of(j * COLUMNS, COLUMNS), COLUMNS)

    def forward(i):
        @pl.loop(0, width // COLUMNS)
        def _(j):
            columns = columns_of(j)
            block = weights[i, :, :, :, :, columns].reshape(width, COLUMNS)
            activation = features_ref[...] if i == 0 else inputs[i - 1]
            summed = jnp.dot(activation, block, preferred_element_type=jnp.float32)
            logistic = jax.nn.sigmoid(summed)
            inputs[i, :, columns] = (summed * logistic).astype(jnp.bfloat16)
            factors[i, :, columns] = logistic * (1.0 + summed * (1.0 - logistic))

    core_copies = [[] for _ in range(layer_count)]

    def send_core(i, place, x_at, source=None):
        slot = len(core_copies[i])
        view = weights.at[i, place, x_at, core]
        core_copies[i].append(
            send(
                view if source is None else source,
                view,
                core_send.at[i, slot],
                core_recv.at[i, slot],
                core_peer,
            )
        )

    for i in range(layer_count):
        send_core(i, z, x, hidden_ref.at[i])
    for i in range(layer_count + 2):
        if i < layer_count:
            for k in range(groups - 1):
                z_copies[i][k].wait_recv()
                send_x(i, k + 1, weights.at[i, z_origins[k], x, core], z_origins[k])
                send_core(i, z_origins[k], x)
            if i + 3 < layer_count:
                send_x(i + 3, 0, hidden_ref.at[i + 3], z)
        if 1 <= i <= layer_count:
            for slot, place in enumerate([z] + z_origins):
                x_copies[i - 1][slot].wait_recv()
                send_core(i - 1, place, 1 - x)
        if i >= 2:
            for copy in core_copies[i - 2]:
                copy.wait_recv()
            forward(i - 2)

    half = batch // 2
    half_rows = pl.ds(pl.multiple_of(core * half, half), half)
    inputs_copy = send_role(inputs.at[last, half_rows, :], got_inputs.at[half_rows, :])
    chunks = [pl.ds(j * COLUMNS, COLUMNS) for j in range(cells // COLUMNS)]
    residual_copies = []
    for columns in chunks:
        predicted = jnp.dot(inputs[last], out_ref[:, columns], preferred_element_type=jnp.float32)
        residual[:, columns] = ((predicted - target_ref[:, columns]) / batch).astype(jnp.bfloat16)
        residual_copies.append(send_role(residual.at[:, columns], got_residual.at[:, columns]))

    parts = [pl.ds(j * COLUMNS, COLUMNS) for j in range(width // COLUMNS)]
    core_sums, x_sums, z_sums, z_slopes, x_slopes, core_slopes = [], [], [], [], [], []
    for j, columns in enumerate(parts):
        part = lax.dot_general(
            residual[...],
            out_ref[columns, :],
            (((1,), (1,)), ((), ())),
            preferred_element_type=jnp.float32,
        )
        partial[:, :, :, :, columns] = part.reshape(groups, 2, 2, rows, COLUMNS)
        core_sums.append(
            send(
                partial.at[:, :, 1 - core, :, columns],
                core_sum.at[:, :, :, columns],
                sum_send.at[j, 0],
                sum_recv.at[j, 0],
                core_peer,
            )
        )
    for j, columns in enumerate(parts):
        core_sums[j].wait_recv()
        away = partial[:, 1 - x, core, :, columns] + core_sum[:, 1 - x, :, columns]
        x_away[:, :, columns] = away.astype(jnp.bfloat16)
        x_sums.append(
            send(
                x_away.at[:, :, columns],
                x_sum.at[:, :, columns],
                sum_send.at[j, 1],
                sum_recv.at[j, 1],
                x_peer,
            )
        )
    for j, columns in enumerate(parts):
        kept = partial[:, x, core, :, columns] + core_sum[:, x, :, columns]
        x_sums[j].wait_recv()
        kept = kept + x_sum[:, :, columns].astype(jnp.float32)
        partial[:, x, core, :, columns] = kept
        z_away[:, :, columns] = kept.astype(jnp.bfloat16)
        z_sums.append(
            [
                send(
                    z_away.at[z_places[k], :, columns],
                    z_sum.at[k, :, columns],
                    sum_send.at[j, 2 + k],
                    sum_recv.at[j, 2 + k],
                    z_peers[k],
                )
                for k in range(groups - 1)
            ]
        )
    own_rows = pl.ds(pl.multiple_of(tile * rows, rows), rows)

    def send_slope(view, j, slot, peer):
        return send(view, view, slope_send.at[j, slot], slope_recv.at[j, slot], peer)

    for j, columns in enumerate(parts):
        upstream = partial[z, x, core, :, columns]
        for k in range(groups - 1):
            z_sums[j][k].wait_recv()
            upstream = upstream + z_sum[k, :, columns].astype(jnp.float32)
        slope[z, x, core, :, columns] = (upstream * factors[last, own_rows, columns]).astype(
            jnp.bfloat16
        )
        view = slope.at[z, x, core, :, columns]
        z_slopes.append([send_slope(view, j, k, z_peers[k]) for k in range(groups - 1)])
    for j, columns in enumerate(parts):
        for copy in z_slopes[j]:
            copy.wait_recv()
        view = slope.at[:, x, core, :, columns]
        x_slopes.append(send_slope(view, j, groups - 1, x_peer))
    for j, columns in enumerate(parts):
        x_slopes[j].wait_recv()
        core_slopes.append(send_slope(slope.at[:, :, core, :, columns], j, groups, core_peer))
    for copy in core_slopes:
        copy.wait_recv()
    for copies in z_slopes + [x_slopes, core_slopes]:
        for copy in copies:
            copy.wait_send()
            sends[:] = [other for other in sends if other is not copy]

    inputs_copy.wait_recv()
    view = got_inputs.at[half_rows, :]
    inputs_swap = send(view, view, local_sem.at[0], local_sem.at[2], core_peer)

    per_block = LANES // unit_rows
    first_lane = pl.multiple_of((tile // per_block) * LANES, LANES)
    unit_first = pl.multiple_of(lax.rem(tile, per_block) * unit_rows, unit_rows)
    for i in reversed(range(layer_count)):
        source = features_ref if i == 0 else inputs.at[i - 1]
        own_inputs = source[:, pl.ds(first_lane, LANES)]

        @pl.loop(0, width // COLUMNS)
        def _(j):
            columns = columns_of(j)
            gradient[:, columns] = lax.dot_general(
                own_inputs,
                slope[:, :, :, :, columns].reshape(batch, COLUMNS),
                (((0,), (0,)), ((), ())),
                preferred_element_type=jnp.float32,
            )

        mine = gradient[pl.ds(unit_first, unit_rows), :].astype(jnp.bfloat16)
        payload_hidden[i] = jnp.where(solver_side, hidden_ref[i], mine)
        if i > 0:
            whole_slope = slope[...].reshape(batch, width)

            @pl.loop(0, width // COLUMNS)
            def _(j):
                columns = columns_of(j)
                block = weights.at[i].reshape(width, width)[columns, :]
                back = lax.dot_general(
                    whole_slope,
                    block,
                    (((1,), (1,)), ((), ())),
                    preferred_element_type=jnp.float32,
                )
                next_slope[:, columns] = (back * factors[i - 1, :, columns]).astype(jnp.bfloat16)

        send_role(payload_hidden.at[i], got_hidden_ref.at[i])
        if i > 0:
            slope[...] = next_slope[...].reshape(slope.shape)
    hidden_keep = pltpu.make_async_copy(payload_hidden, sent_hidden_ref, local_sem.at[1])
    hidden_keep.start()
    inputs_swap.wait_recv()
    for copy in residual_copies:
        copy.wait_recv()
    chosen = jnp.where(solver_side, got_inputs[...], inputs[last])
    keeps = [hidden_keep]
    for j, columns in enumerate(chunks):
        grad = lax.dot_general(
            chosen,
            jnp.where(solver_side, got_residual[:, columns], residual[:, columns]),
            (((0,), (0,)), ((), ())),
            preferred_element_type=jnp.float32,
        )
        payload[:, columns] = grad.astype(jnp.bfloat16)
        keep = pltpu.make_async_copy(
            payload.at[:, columns], grad_out_ref.at[:, columns], local_sem.at[4 + j]
        )
        keep.start()
        keeps.append(keep)
    waited = [inputs_copy] + residual_copies
    for copy in role_copies:
        if not any(copy is other for other in waited):
            copy.wait_recv()
    for copy in sends:
        copy.wait_send()
    for keep in keeps:
        keep.wait()


def fused_training(features, hidden_narrow, out_narrow, own_fields, own_out, own_hidden, fields):
    layer_count, unit_rows, width = hidden_narrow.shape
    batch, cells = own_fields.shape
    groups = lax.axis_size("tile") // 4
    rows = batch // lax.axis_size("tile")
    narrow, wide = jnp.bfloat16, jnp.float32
    dma = pltpu.SemaphoreType.DMA
    vmem = pl.BlockSpec(memory_space=pltpu.VMEM)
    anywhere = pl.BlockSpec(memory_space=pl.ANY)
    parts = width // COLUMNS
    role_slots = 3 + cells // COLUMNS + layer_count
    return pl.pallas_call(
        functools.partial(train_kernel, groups),
        out_shape=(
            jax.ShapeDtypeStruct((width, cells), narrow),
            jax.ShapeDtypeStruct(hidden_narrow.shape, narrow),
            jax.ShapeDtypeStruct((width, cells), narrow),
            jax.ShapeDtypeStruct(hidden_narrow.shape, narrow),
            jax.ShapeDtypeStruct((batch, cells), narrow),
        ),
        in_specs=[anywhere, vmem] + [anywhere] * 3,
        out_specs=[anywhere] * 5,
        scratch_shapes=[
            pltpu.VMEM((batch, width), narrow),
            pltpu.VMEM((width, cells), narrow),
            pltpu.VMEM((batch, cells), wide),
            pltpu.VMEM((layer_count, groups, 2, 2, unit_rows, width), narrow),
            pltpu.VMEM((layer_count, batch, width), narrow),
            pltpu.VMEM((layer_count, batch, width), wide),
            pltpu.VMEM((batch, cells), narrow),
            pltpu.VMEM((batch, width), narrow),
            pltpu.VMEM((batch, cells), narrow),
            pltpu.VMEM((batch, width), narrow),
            pltpu.VMEM((groups, 2, 2, rows, width), wide),
            pltpu.VMEM((groups, 2, 2, rows, width), narrow),
            pltpu.VMEM((width, cells), narrow),
            pltpu.VMEM(hidden_narrow.shape, narrow),
            pltpu.VMEM((LANES, width), wide),
            pltpu.VMEM((groups, 2, rows, width), wide),
            pltpu.VMEM((groups, rows, width), narrow),
            pltpu.VMEM((groups, rows, width), narrow),
            pltpu.VMEM((groups, rows, width), narrow),
            pltpu.VMEM((groups - 1, rows, width), narrow),
            dma((layer_count, groups - 1)),
            dma((layer_count, groups - 1)),
            dma((layer_count, groups)),
            dma((layer_count, groups)),
            dma((layer_count, 2 * groups)),
            dma((layer_count, 2 * groups)),
            dma((parts, groups + 1)),
            dma((parts, groups + 1)),
            dma((parts, groups + 1)),
            dma((parts, groups + 1)),
            dma((role_slots,)),
            dma((role_slots,)),
            dma((4 + cells // COLUMNS,)),
        ],
        compiler_params=pltpu.CompilerParams(
            collective_id=0, has_side_effects=True, vmem_limit_bytes=64000000
        ),
        cost_estimate=pl.CostEstimate(
            flops=60 * batch * width * width, bytes_accessed=40 * batch * width, transcendentals=0
        ),
    )(features, hidden_narrow, out_narrow, own_fields, fields)


def training(features, hidden_narrow, out_narrow, own_fields, own_out, own_hidden, fields):
    tiles = lax.axis_size("tile")
    fits = (
        tiles % 4 == 0
        and tiles > 4
        and (own_fields.shape[0] // tiles) % 16 == 0
        and LANES % own_hidden.shape[1] == 0
    )
    chosen = fused_training if fits else plain_training
    return chosen(features, hidden_narrow, out_narrow, own_fields, own_out, own_hidden, fields)


def body(fields_pair, velocity, growth, features, assignment, out_pair, hidden_pair):
    solver_side = lax.axis_index("role") == 0
    own_fields = fields_pair[0]
    own_out = out_pair[0]
    own_hidden = hidden_pair[0]
    stacked = jnp.concatenate([own_fields, velocity[None, :]], axis=0)
    advanced = advance(extended(stacked, "tile", 1, 1), growth)
    grad_out, grad_hidden, other_out, other_hidden, fresh_fields = training(
        features,
        own_hidden.astype(jnp.bfloat16),
        own_out.astype(jnp.bfloat16),
        own_fields,
        own_out,
        own_hidden,
        advanced.astype(jnp.bfloat16),
    )
    grad_out, grad_hidden, other_out, other_hidden = (
        v.astype(jnp.float32) for v in (grad_out, grad_hidden, other_out, other_hidden)
    )
    out_next = jnp.where(
        solver_side,
        momentum_decay * own_out + grad_out,
        own_out - step_size * (momentum_decay * other_out + grad_out),
    )
    hidden_next = jnp.where(
        solver_side,
        momentum_decay * own_hidden + other_hidden,
        own_hidden - step_size * (momentum_decay * other_hidden + grad_hidden),
    )
    next_batch = jnp.take(fresh_fields, assignment, axis=0).astype(jnp.float32)
    fields_next = jnp.where(solver_side, advanced, next_batch)
    return (fields_next[None], out_next[None], hidden_next[None])


def solution(mesh):
    return jax.shard_map(
        body,
        mesh=mesh,
        in_specs=(
            P("role", None, "tile"),
            P("tile"),
            P("tile"),
            P(),
            P(),
            P("role", None, "tile"),
            P("role", None, "tile", None),
        ),
        out_specs=(P("role", None, "tile"), P("role", None, "tile"), P("role", None, "tile", None)),
        check_vma=False,
    )
```

profile of v0, /device:TPU:0, one launch (start us, length us, event | category | flops | bytes accessed | tf_op | source)
XLA Modules:
  0.0 158.8 jit_solution(14964906275522872902)
XLA Ops:
  0.6 0.0 copy-start.8
  0.6 0.0 copy-start.1
  0.7 1.3 pad_maximum_fusion.5
  2.0 5.5 %collective-permute-start.1 = (f32[513,1]{1,0:T(8,128)S(1)}, f32[513,1]{1,0:T(8,128)S(1)}, u32[]{:S(2)}, u32[]{:S(2)}) collective-permute-start(f32[513,1]{1,0:T(8,128)S(1)} %get-tuple-element.18), channel_id=1, source_target_pairs={{1,0},{2,1},{3,2},{4,3},{5,4},{6,5},{7,6},{8,7},{9,8},{10,9},{11,1... | collective-permute-start | bytes 6164 | tf_op jit(solution)/shard_map/ppermute | solution.py:21
  7.5 0.0 collective-permute-start
  7.5 0.0 copy-done.8
  7.5 2.3 %bitcast_convert_fusion.1.hidden_ref = bf16[5,64,1024]{2,1,0:T(8,128)(2,1)} fusion(f32[1,5,64,1024]{3,2,1,0:T(8,128)} %param.13), kind=kLoop, calls=%fused_computation.28 | loop fusion | flops 327680 | bytes 1966080 | tf_op jit(solution)/shard_map/convert_element_type | solution.py:529
  9.8 0.0 copy-done.1
  9.8 0.0 copy-start
  9.8 0.0 copy-start.7
  9.8 1.6 %bitcast_convert_fusion.out_hbm = bf16[1024,1024]{1,0:T(8,128)(2,1)} fusion(f32[1,1024,1024]{2,1,0:T(8,128)S(1)} %copy-done.1), kind=kLoop, calls=%fused_computation.8 | loop fusion | flops 1048576 | bytes 6291456 | tf_op jit(solution)/shard_map/convert_element_type | solution.py:530
  11.5 4.6 %collective-permute-done = f32[513,1]{1,0:T(8,128)S(1)} collective-permute-done((f32[513,1]{1,0:T(8,128)S(1)}, f32[513,1]{1,0:T(8,128)S(1)}, u32[]{:S(2)}, u32[]{:S(2)}) %collective-permute-start) | collective-permute-done | bytes 2084 | tf_op jit(solution)/shard_map/ppermute | solution.py:20
  16.0 0.0 copy-done
  16.0 0.0 copy-done.7
  16.0 0.1 maximum_reduce_fusion
  16.2 0.0 collective-permute-done.1
  16.2 0.0 copy-start.9
  16.2 0.7 fusion.5
  16.9 0.0 copy-done.9
  16.9 2.4 %fusion.12 = (bf16[512,1024]{1,0:T(8,128)(2,1)}, f32[512,1024]{1,0:T(8,128)}) fusion(f32[1024]{0:T(1024)S(1)} %copy-done.9, f32[512,1025]{1,0:T(8,128)S(1)} %fusion.5, f32[1,512,1024]{2,1,0:T(8,128)S(1)} %copy-done), kind=kLoop, calls=%fused_computation.37 | loop fusion | flops 3670016 | bytes 9441280 | tf_op jit(solution)/shard_map/convert_element_type | solution.py:534
  19.3 125.2 %shard_map.94 = (bf16[1024,1024]{1,0:T(8,128)(2,1)}, bf16[5,64,1024]{2,1,0:T(8,128)(2,1)}, bf16[1024,1024]{1,0:T(8,128)(2,1)}, bf16[5,64,1024]{2,1,0:T(8,128)(2,1)}, bf16[512,1024]{1,0:T(8,128)(2,1)}) custom-call(bf16[512,1024]{1,0:T(8,128)(2,1)} %features_hbm.1, bf16[5,64,1024]{2,1,0:T(8,128)(2,1)} %bitcast_convert_fusion.1.hidden_ref, ...), custom_call_target="tpu_custom_call" | custom-call | flops 32212254720 | bytes 20971520 | tf_op jit(solution)/shard_map/pallas_call | solution.py:453
  144.5 0.0 copy-start.4
  144.5 4.2 %gather_fusion = bf16[512,1024]{1,0:T(8,128)(2,1)S(1)} fusion(bf16[512,1024]{1,0:T(8,128)(2,1)} %get-tuple-element.8, s32[1024]{0:T(1024)S(1)} %pad_clamp_fusion), kind=kCustom, calls=%fused_computation | custom fusion | bytes 2099200 | tf_op jit(solution)/shard_map/jit(_take)/gather | solution.py:549
  148.8 0.0 copy-done.4
  148.8 0.0 copy-start.3
  148.8 0.0 copy-start.5
  148.8 0.0 copy-start.6
  148.8 6.3 %fusion.1 = f32[1,1024,1024]{2,1,0:T(8,128)} fusion(bf16[1024,1024]{1,0:T(8,128)(2,1)S(1)} %copy-done.4, f32[1,1024,1024]{2,1,0:T(8,128)} %param.12, bf16[1024,1024]{1,0:T(8,128)(2,1)} %get-tuple-element.10, pred[]{:T(512)S(6)} %eq.3), kind=kLoop, calls=%fused_computation.4 | loop fusion | flops 9437184 | bytes 12582913 | tf_op jit(solution)/shard_map/broadcast_in_dim | solution.py:551
  155.1 0.0 copy-start.2
  155.2 0.0 copy-done.3
  155.2 0.0 copy-done.5
  155.2 0.0 copy-done.6
  155.2 1.5 fusion.8
  156.6 0.6 copy-done.2
  157.2 1.6 %select_bitcast_fusion = f32[1,512,1024]{2,1,0:T(8,128)} fusion(f32[512,1024]{1,0:T(8,128)S(1)} %copy-done.2, bf16[512,1024]{1,0:T(8,128)(2,1)S(1)} %gather_fusion, pred[512]{0:T(512)(128)(4,1)S(1)} %compare_and_fusion, pred[]{:T(512)S(6)} %eq.3), kind=kLoop, calls=%fused_computation.18 | loop fusion | flops 1572864 | bytes 5243393 | tf_op jit(solution)/shard_map/broadcast_in_dim | solution.py:551
  (3 shorter events, 0.0 us)
Async XLA Ops:
  0.6 6.9 %copy-start.8 = (s32[512]{0:T(512)S(1)}, s32[512]{0:T(512)}, u32[]{:S(2)}) copy-start(s32[512]{0:T(512)} %param.11) | copy-start | bytes 6148
  0.6 9.2 %copy-start.1 = (f32[1,1024,1024]{2,1,0:T(8,128)S(1)}, f32[1,1024,1024]{2,1,0:T(8,128)}, u32[]{:S(2)}) copy-start(f32[1,1024,1024]{2,1,0:T(8,128)} %param.12) | copy-start | bytes 12582916
  2.0 14.1 %collective-permute-start.1 = (f32[513,1]{1,0:T(8,128)S(1)}, f32[513,1]{1,0:T(8,128)S(1)}, u32[]{:S(2)}, u32[]{:S(2)}) collective-permute-start(f32[513,1]{1,0:T(8,128)S(1)} %get-tuple-element.18), channel_id=1, source_target_pairs={{1,0},{2,1},{3,2},{4,3},{5,4},{6,5},{7,6},{8,7},{9,8},{10,9},{11,1... | collective-permute-start | bytes 6164 | tf_op jit(solution)/shard_map/ppermute | solution.py:21
  7.5 8.5 %collective-permute-start = (f32[513,1]{1,0:T(8,128)S(1)}, f32[513,1]{1,0:T(8,128)S(1)}, u32[]{:S(2)}, u32[]{:S(2)}) collective-permute-start(f32[513,1]{1,0:T(8,128)S(1)} %get-tuple-element.17), channel_id=1, source_target_pairs={{0,1},{1,2},{2,3},{3,4},{4,5},{5,6},{6,7},{7,8},{8,9},{9,10},{10,1... | collective-permute-start | bytes 6164 | tf_op jit(solution)/shard_map/ppermute | solution.py:20
  9.8 6.2 %copy-start = (f32[1,512,1024]{2,1,0:T(8,128)S(1)}, f32[1,512,1024]{2,1,0:T(8,128)}, u32[]{:S(2)}) copy-start(f32[1,512,1024]{2,1,0:T(8,128)} %param.7) | copy-start | bytes 6291460
  9.8 6.2 %copy-start.7 = (f32[1024]{0:T(1024)S(1)}, f32[1024]{0:T(1024)}, u32[]{:S(2)}) copy-start(f32[1024]{0:T(1024)} %param.8) | copy-start | bytes 12292
  16.2 0.7 copy-start.9
  144.5 4.3 %copy-start.4 = (bf16[1024,1024]{1,0:T(8,128)(2,1)S(1)}, bf16[1024,1024]{1,0:T(8,128)(2,1)}, u32[]{:S(2)}) copy-start(bf16[1024,1024]{1,0:T(8,128)(2,1)} %get-tuple-element.9) | copy-start | bytes 6291460
  148.8 6.4 %copy-start.3 = (f32[1,5,64,1024]{3,2,1,0:T(8,128)S(1)}, f32[1,5,64,1024]{3,2,1,0:T(8,128)}, u32[]{:S(2)}) copy-start(f32[1,5,64,1024]{3,2,1,0:T(8,128)} %param.13) | copy-start | bytes 3932164
  148.8 6.3 %copy-start.5 = (bf16[5,64,1024]{2,1,0:T(8,128)(2,1)S(1)}, bf16[5,64,1024]{2,1,0:T(8,128)(2,1)}, u32[]{:S(2)}) copy-start(bf16[5,64,1024]{2,1,0:T(8,128)(2,1)} %get-tuple-element.12) | copy-start | bytes 1966084
  148.8 6.3 %copy-start.6 = (bf16[5,64,1024]{2,1,0:T(8,128)(2,1)S(1)}, bf16[5,64,1024]{2,1,0:T(8,128)(2,1)}, u32[]{:S(2)}) copy-start(bf16[5,64,1024]{2,1,0:T(8,128)(2,1)} %get-tuple-element.11) | copy-start | bytes 1966084
  155.1 2.1 %copy-start.2 = (f32[512,1024]{1,0:T(8,128)S(1)}, f32[512,1024]{1,0:T(8,128)}, u32[]{:S(2)}) copy-start(f32[512,1024]{1,0:T(8,128)} %get-tuple-element.16) | copy-start | bytes 6291460
where the time goes:
time: 159 us
  Pallas kernels  125 us (79%)
  other arithmetic  17.9 us (11%)
  starting transfers between devices  5.5 us (3%)
  local copies, waits for them, and re-layouts  4.87 us (3%)
  waiting for transfers between devices  4.56 us (3%)
    pallas_call x1, Pallas kernels, fused_training(): pl.pallas_call(functools.partial(train_kernel, groups), out_shape=(jax.Sh...  125 us
    broadcast_in_dim x3, other arithmetic, body(): return (fields_next[None], out_next[None], hidden_next[None])  9.4 us
    ppermute x1, starting transfers between devices, extended(): after = lax.ppermute(leading, axis, down)  5.5 us
    ppermute x1, waiting for transfers between devices, extended(): before = lax.ppermute(last, axis, up)  4.55 us
    gather x1, local copies, waits for them, and re-layouts, body(): next_batch = jnp.take(fresh_fields, assignment, axis=0).astype(jnp.float32)  4.24 us
  transfers between devices with their start and end apart: 2, of which 1 were waited for; matrix products, arithmetic and copies ran while one was open for 3% of the time, Pallas kernels for 0%

commit v1 on v0

v1 whole, which is shorter than its diff:
```python
import functools

import jax
import jax.numpy as jnp
from jax import lax
from jax.experimental import pallas as pl
from jax.experimental.pallas import tpu as pltpu
from jax.sharding import PartitionSpec as P

momentum_decay = 0.9
step_size = 0.1


def extended(value, axis, dim, width):
    count, length = (lax.axis_size(axis), value.shape[dim])
    up = [(i, (i + 1) % count) for i in range(count)]
    down = [(j, i) for i, j in up]
    last = lax.slice_in_dim(value, length - width, length, axis=dim)
    leading = lax.slice_in_dim(value, 0, width, axis=dim)
    before = lax.ppermute(last, axis, up)
    after = lax.ppermute(leading, axis, down)
    return jnp.concatenate([before, value, after], axis=dim)


def silu_slope(values):
    logistic = jax.nn.sigmoid(values)
    return logistic * (1.0 + values * (1.0 - logistic))


def advance(padded, growth):
    states = padded[:-1]
    velocity_row = padded[-1]
    outflow = (
        jnp.maximum(velocity_row[:-1], 0.0) * states[:, :-1]
        + jnp.minimum(velocity_row[:-1], 0.0) * states[:, 1:]
    )
    carried = states[:, 1:-1] - outflow[:, 1:] + outflow[:, :-1]
    return carried + growth * carried * (1.0 - carried)


def to_trainer(value):
    return lax.ppermute(value.astype(jnp.bfloat16), "role", [(0, 1)])


def to_solver(value):
    return lax.ppermute(value.astype(jnp.bfloat16), "role", [(1, 0)])


def plain_training(features, hidden_narrow, out_narrow, own_fields, own_out, own_hidden, fields):
    layer_count, unit_rows = own_hidden.shape[:2]
    batch = own_fields.shape[0]
    first_unit = lax.axis_index("tile") * unit_rows
    momentum_out = to_trainer(own_out)
    momentum_hidden = to_trainer(own_hidden)
    full_hidden = [
        lax.all_gather(hidden_narrow[i], "tile", axis=0, tiled=True) for i in range(layer_count)
    ]
    inputs, summed_list = [], []
    activation = features
    for i in range(layer_count):
        inputs.append(activation)
        summed = jnp.dot(activation, full_hidden[i], preferred_element_type=jnp.float32)
        summed_list.append(summed)
        activation = jax.nn.silu(summed).astype(jnp.bfloat16)
    predicted = jnp.dot(activation, out_narrow, preferred_element_type=jnp.float32)
    residual = ((predicted - own_fields) / batch).astype(jnp.bfloat16)
    partial_grad = lax.dot_general(
        residual, out_narrow, (((1,), (1,)), ((), ())), preferred_element_type=jnp.float32
    )
    upstream = lax.psum(partial_grad, "tile")
    grad_out = jnp.dot(activation.T, residual, preferred_element_type=jnp.float32)
    sent_out = to_solver(grad_out)
    gradients, sent = [], []
    for i in reversed(range(layer_count)):
        slope = (upstream * silu_slope(summed_list[i])).astype(jnp.bfloat16)
        own_inputs = lax.dynamic_slice_in_dim(inputs[i], first_unit, unit_rows, 1)
        gradient = jnp.dot(own_inputs.T, slope, preferred_element_type=jnp.float32)
        gradients.append(gradient)
        sent.append(to_solver(gradient))
        if i > 0:
            upstream = lax.dot_general(
                slope, full_hidden[i], (((1,), (1,)), ((), ())), preferred_element_type=jnp.float32
            )
    solver_side = lax.axis_index("role") == 0
    grad_out = jnp.where(solver_side, sent_out.astype(jnp.float32), grad_out)
    other_hidden = jnp.where(solver_side, jnp.stack(sent[::-1]), momentum_hidden)
    return grad_out, jnp.stack(gradients[::-1]), momentum_out, other_hidden, to_trainer(fields)


LANES = 128
COLUMNS = 256


class Later:
    def __init__(self, build):
        self.build = build

    def start(self):
        self.build().start()

    def wait(self):
        self.build().wait()

    def wait_recv(self):
        self.build().wait_recv()

    def wait_send(self):
        self.build().wait_send()


def train_kernel(
    groups,
    features_hbm,
    fields_hbm,
    velocity_hbm,
    growth_hbm,
    assignment_hbm,
    out_hbm,
    hidden_hbm,
    fields_next,
    out_next,
    hidden_next,
    features_ref,
    own_fields,
    own_out,
    own_hidden,
    velocity_ref,
    growth_ref,
    assignment_ref,
    left_velocity,
    left_edge,
    right_edge,
    out_ref,
    got_out,
    got_hidden,
    got_fields,
    weights,
    inputs,
    factors,
    residual,
    slope_even,
    slope_odd,
    partial,
    slope,
    gradient,
    core_sum,
    x_away,
    x_sum,
    z_away,
    z_sum,
    z_send,
    z_recv,
    x_send,
    x_recv,
    core_send,
    core_recv,
    sum_send,
    sum_recv,
    slope_send,
    slope_recv,
    role_send,
    role_recv,
    edge_send,
    edge_recv,
    local_sem,
    keep_sem,
):
    layer_count, unit_rows, width = hidden_hbm.shape
    batch, cells = fields_hbm.shape
    rows = partial.shape[3]
    narrow, wide = jnp.bfloat16, jnp.float32
    tiles = groups * 4
    last = layer_count - 1
    role = lax.axis_index("role")
    tile = lax.axis_index("tile")
    core = lax.rem(tile, 2)
    x = lax.rem(tile // 2, 2)
    z = tile // 4
    solver = role == 0
    trainer = role == 1

    def device(z_at, x_at, core_at):
        return (role, z_at * 4 + x_at * 2 + core_at)

    z_places = [lax.rem(z + k, groups) for k in range(1, groups)]
    z_origins = [lax.rem(z + groups - k, groups) for k in range(1, groups)]
    z_peers = [device(place, x, core) for place in z_places]
    x_peer = device(z, 1 - x, core)
    core_peer = device(z, x, 1 - core)
    role_peer = (1 - role, tile)
    right_peer = (role, lax.rem(tile + 1, tiles))
    left_peer = (role, lax.rem(tile + tiles - 1, tiles))
    far_peer = (role, lax.rem(tile + tiles - 1 + 2 * core, tiles))
    sends, solver_sends, trainer_sends = [], [], []

    def remote(views, semaphores, slot, peer):
        def build():
            source, target = views()
            return pltpu.make_async_remote_copy(
                src_ref=source,
                dst_ref=target,
                send_sem=semaphores[0].at[slot],
                recv_sem=semaphores[1].at[slot],
                device_id=peer,
                device_id_type=pl.DeviceIdType.MESH,
            )

        return Later(build)

    def local(views, semaphores, slot):
        def build():
            source, target = views()
            return pltpu.make_async_copy(source, target, semaphores.at[slot])

        return Later(build)

    def twice(view):
        return lambda: (view(),) * 2

    def start(copy, among):
        copy.start()
        among.append(copy)
        return copy

    role_slots = [0]

    def across(view):
        slot = role_slots[0]
        role_slots[0] += 1
        return remote(twice(view), (role_send, role_recv), slot, role_peer)

    chunks = [pl.ds(j * COLUMNS, COLUMNS) for j in range(cells // COLUMNS)]
    parts = [pl.ds(j * COLUMNS, COLUMNS) for j in range(width // COLUMNS)]
    shares = [across(lambda i=i: weights.at[i, z, x, core]) for i in range(layer_count)]
    momenta = [across(lambda c=c: got_out.at[:, c]) for c in chunks]
    hidden_momentum = across(lambda: got_hidden)
    fresh = [across(lambda c=c: got_fields.at[:, c]) for c in chunks]
    residuals = [across(lambda c=c: residual.at[:, c]) for c in chunks]
    slope_shares = [across(lambda c=c: slope.at[z, x, core, :, c]) for c in parts]

    kept = [lambda c=c: (own_fields.at[:, c], fields_next.at[:, c]) for c in chunks]
    kept += [lambda c=c: (own_out.at[:, c], out_next.at[:, c]) for c in chunks]
    kept += [lambda: (own_hidden, hidden_next)]
    keeps = [local(views, keep_sem, k) for k, views in enumerate(kept)]
    keep_fields, keep_out = keeps[: len(chunks)], keeps[len(chunks) : -1]
    keep_hidden = keeps[-1]

    pairs = [lambda: (hidden_hbm, own_hidden)]
    pairs += [lambda c=c: (out_hbm.at[:, c], own_out.at[:, c]) for c in chunks]
    pairs += [
        lambda: (fields_hbm, own_fields),
        lambda: (velocity_hbm, velocity_ref),
        lambda: (growth_hbm, growth_ref),
        lambda: (assignment_hbm, assignment_ref),
        lambda: (features_hbm, features_ref),
    ]
    loads = [local(views, local_sem, k) for k, views in enumerate(pairs)]
    for load in loads:
        load.start()
    hidden_load, out_loads, small_loads = loads[0], loads[1 : 1 + len(chunks)], loads[1 + len(chunks) :]
    barrier = pltpu.get_barrier_semaphore()
    peers = z_peers + [x_peer, core_peer, role_peer, far_peer]
    for peer in peers:
        pl.semaphore_signal(barrier, inc=1, device_id=peer, device_id_type=pl.DeviceIdType.MESH)
    pl.semaphore_wait(barrier, len(peers))

    last_lanes = pl.ds(cells - LANES, LANES)
    edge_list = [
        (lambda: (fields_hbm.at[:, last_lanes], left_edge), right_peer),
        (lambda: (velocity_hbm.at[:, last_lanes], left_velocity), right_peer),
        (lambda: (fields_hbm.at[:, pl.ds(0, LANES)], right_edge), left_peer),
    ]
    edges = [
        remote(views, (edge_send, edge_recv), k, peer) for k, (views, peer) in enumerate(edge_list)
    ]

    z_copies = []
    x_copies = [[] for _ in range(layer_count)]
    core_copies = [[] for _ in range(layer_count)]

    def send_x(i, slot, place):
        view = twice(lambda: weights.at[i, place, x, core])
        copy = remote(view, (x_send, x_recv), (i, slot), x_peer)
        x_copies[i].append(start(copy, sends))

    def send_core(i, place, x_at):
        slot = len(core_copies[i])
        view = twice(lambda: weights.at[i, place, x_at, core])
        copy = remote(view, (core_send, core_recv), (i, slot), core_peer)
        core_copies[i].append(start(copy, sends))

    def send_share(i):
        @pl.when(solver)
        def _():
            shares[i].wait_recv()

        view = twice(lambda: weights.at[i, z, x, core])
        z_copies.append(
            [
                start(remote(view, (z_send, z_recv), (i, k), z_peers[k]), sends)
                for k in range(groups - 1)
            ]
        )
        send_x(i, 0, z)
        send_core(i, z, x)

    def columns_of(j):
        return pl.ds(pl.multiple_of(j * COLUMNS, COLUMNS), COLUMNS)

    def advance():
        velocity = velocity_ref[...]
        forward_speed = jnp.maximum(velocity, 0.0)
        backward_speed = jnp.minimum(velocity, 0.0)
        growth = growth_ref[...]
        before = left_velocity[:, LANES - 1 :]
        step = LANES // 2

        @pl.loop(0, batch // step)
        def _(j):
            band = pl.ds(pl.multiple_of(j * step, step), step)
            current = own_fields[band, :]
            lane = lax.broadcasted_iota(jnp.int32, current.shape, 1)
            following = jnp.where(
                lane == cells - 1, right_edge[band, :1], pltpu.roll(current, cells - 1, 1)
            )
            outflow = forward_speed * current + backward_speed * following
            inflow_edge = (
                jnp.maximum(before, 0.0) * left_edge[band, :][:, LANES - 1 :]
                + jnp.minimum(before, 0.0) * current[:, :1]
            )
            inflow = jnp.where(lane == 0, inflow_edge, pltpu.roll(outflow, 1, 1))
            carried = current - outflow + inflow
            advanced = carried + growth * carried * (1.0 - carried)
            own_fields[band, :] = advanced
            got_fields[band, :] = advanced.astype(narrow)

    @pl.when(solver)
    def _():
        for copy in edges:
            start(copy, solver_sends)
        for load, c, copy in zip(out_loads, chunks, momenta):
            load.wait()
            got_out[:, c] = own_out[:, c].astype(narrow)
            start(copy, solver_sends)
        hidden_load.wait()
        got_hidden[...] = own_hidden[...].astype(narrow)
        start(hidden_momentum, solver_sends)

    @pl.when(trainer)
    def _():
        hidden_load.wait()
        for i in range(layer_count):
            weights[i, z, x, core] = own_hidden[i].astype(narrow)
            start(shares[i], trainer_sends)

    send_share(0)
    send_share(1)

    for load in small_loads:
        load.wait()

    @pl.when(solver)
    def _():
        for copy in edges:
            copy.wait_recv()
        advance()
        for copy, written in zip(fresh, keep_fields):
            start(copy, solver_sends)
            written.start()

    @pl.when(trainer)
    def _():
        for load, c in zip(out_loads, chunks):
            load.wait()
            out_ref[:, c] = own_out[:, c].astype(narrow)

    def forward(i):
        @pl.loop(0, width // COLUMNS)
        def _(j):
            columns = columns_of(j)
            block = weights[i, :, :, :, :, columns].reshape(width, COLUMNS)
            activation = features_ref[...] if i == 0 else inputs[i - 1]
            summed = jnp.dot(activation, block, preferred_element_type=wide)
            logistic = jax.nn.sigmoid(summed)
            inputs[i, :, columns] = (summed * logistic).astype(narrow)
            factors[i, :, columns] = logistic * (1.0 + summed * (1.0 - logistic))

    for i in range(layer_count + 2):
        if i + 2 < layer_count:
            send_share(i + 2)
        if i < layer_count:
            for k in range(groups - 1):
                z_copies[i][k].wait_recv()
                send_x(i, k + 1, z_origins[k])
                send_core(i, z_origins[k], x)
        if 1 <= i <= layer_count:
            for slot, place in enumerate([z] + z_origins):
                x_copies[i - 1][slot].wait_recv()
                send_core(i - 1, place, 1 - x)
        if i >= 2:
            for copy in core_copies[i - 2]:
                copy.wait_recv()
            forward(i - 2)

    def update_out(j, decay, rate, other):
        c = chunks[j]

        @pl.loop(0, width // COLUMNS)
        def _(k):
            units = columns_of(k)
            grad = lax.dot_general(
                inputs[last, :, units],
                residual[:, c],
                (((0,), (0,)), ((), ())),
                preferred_element_type=wide,
            )
            if other is None:
                own_out[units, c] = decay * own_out[units, c] + grad
            else:
                fresh_momentum = decay * other[units, c].astype(wide) + grad
                own_out[units, c] = own_out[units, c] - rate * fresh_momentum

        keep_out[j].start()

    def update_solver(j):
        residuals[j].wait_recv()
        update_out(j, momentum_decay, None, None)

    def update_trainer(j):
        momenta[j].wait_recv()
        update_out(j, momentum_decay, step_size, got_out)

    core_sums, x_sums, z_sums, z_slopes, x_slopes, core_slopes = [], [], [], [], [], []

    def send_sum(views, j, slot, peer):
        return start(remote(views, (sum_send, sum_recv), (j, slot), peer), trainer_sends)

    @pl.when(trainer)
    def _():
        for j, c in enumerate(chunks):
            predicted = jnp.dot(inputs[last], out_ref[:, c], preferred_element_type=wide)
            residual[:, c] = ((predicted - own_fields[:, c]) / batch).astype(narrow)
            if j + 1 < len(chunks):
                start(residuals[j], trainer_sends)
        for j, columns in enumerate(parts):
            part = lax.dot_general(
                residual[...],
                out_ref[columns, :],
                (((1,), (1,)), ((), ())),
                preferred_element_type=wide,
            )
            partial[:, :, :, :, columns] = part.reshape(groups, 2, 2, rows, COLUMNS)
            core_sums.append(
                send_sum(
                    lambda columns=columns: (
                        partial.at[:, :, 1 - core, :, columns],
                        core_sum.at[:, :, :, columns],
                    ),
                    j,
                    0,
                    core_peer,
                )
            )
        for j, columns in enumerate(parts):
            core_sums[j].wait_recv()
            away = partial[:, 1 - x, core, :, columns] + core_sum[:, 1 - x, :, columns]
            x_away[:, :, columns] = away.astype(narrow)
            x_sums.append(
                send_sum(
                    lambda columns=columns: (x_away.at[:, :, columns], x_sum.at[:, :, columns]),
                    j,
                    1,
                    x_peer,
                )
            )
        update_trainer(0)
        for j, columns in enumerate(parts):
            near = partial[:, x, core, :, columns] + core_sum[:, x, :, columns]
            x_sums[j].wait_recv()
            near = near + x_sum[:, :, columns].astype(wide)
            partial[:, x, core, :, columns] = near
            z_away[:, :, columns] = near.astype(narrow)
            z_sums.append(
                [
                    send_sum(
                        lambda columns=columns, k=k: (
                            z_away.at[z_places[k], :, columns],
                            z_sum.at[k, :, columns],
                        ),
                        j,
                        2 + k,
                        z_peers[k],
                    )
                    for k in range(groups - 1)
                ]
            )
        update_trainer(1)

    @pl.when(solver)
    def _():
        update_solver(0)
        update_solver(1)

    own_rows = pl.ds(pl.multiple_of(tile * rows, rows), rows)

    def send_slope(view, j, slot, peer):
        return start(remote(twice(view), (slope_send, slope_recv), (j, slot), peer), sends)

    for j, columns in enumerate(parts):

        @pl.when(trainer)
        def _():
            upstream = partial[z, x, core, :, columns]
            for k in range(groups - 1):
                z_sums[j][k].wait_recv()
                upstream = upstream + z_sum[k, :, columns].astype(wide)
            slope[z, x, core, :, columns] = (upstream * factors[last, own_rows, columns]).astype(
                narrow
            )
            start(slope_shares[j], trainer_sends)

        @pl.when(solver)
        def _():
            slope_shares[j].wait_recv()

        view = lambda columns=columns: slope.at[z, x, core, :, columns]
        z_slopes.append([send_slope(view, j, k, z_peers[k]) for k in range(groups - 1)])

    @pl.when(trainer)
    def _():
        start(residuals[-1], trainer_sends)
        update_trainer(2)

    for j, columns in enumerate(parts):
        for copy in z_slopes[j]:
            copy.wait_recv()
        x_slopes.append(send_slope(
            lambda columns=columns: slope.at[:, x, core, :, columns], j, groups - 1, x_peer
        ))
    for j, columns in enumerate(parts):
        x_slopes[j].wait_recv()
        core_slopes.append(send_slope(
            lambda columns=columns: slope.at[:, :, core, :, columns], j, groups, core_peer
        ))

    @pl.when(trainer)
    def _():
        update_trainer(3)
        hidden_momentum.wait_recv()

    for copy in core_slopes:
        copy.wait_recv()

    per_block = LANES // unit_rows
    first_lane = pl.multiple_of((tile // per_block) * LANES, LANES)
    unit_first = pl.multiple_of(lax.rem(tile, per_block) * unit_rows, unit_rows)
    slopes = [slope.reshape(batch, width), slope_even, slope_odd]
    for step, i in enumerate(reversed(range(layer_count))):
        source = features_ref if i == 0 else inputs.at[i - 1]
        this_slope = slopes[0] if step == 0 else slopes[1 + step % 2]
        next_slope = slopes[1 + (step + 1) % 2]
        if i > 0:

            @pl.loop(0, width // COLUMNS)
            def _(j):
                columns = columns_of(j)
                block = weights.at[i].reshape(width, width)[columns, :]
                back = lax.dot_general(
                    this_slope[...],
                    block,
                    (((1,), (1,)), ((), ())),
                    preferred_element_type=wide,
                )
                next_slope[:, columns] = (back * factors[i - 1, :, columns]).astype(narrow)

        @pl.loop(0, width // COLUMNS)
        def _(j):
            columns = columns_of(j)
            gradient[:, columns] = lax.dot_general(
                source[:, pl.ds(first_lane, LANES)],
                this_slope[:, columns],
                (((0,), (0,)), ((), ())),
                preferred_element_type=wide,
            )

        own_units = pl.ds(unit_first, unit_rows)

        @pl.when(solver)
        def _():
            own_hidden[i] = momentum_decay * own_hidden[i] + gradient[own_units, :]

        @pl.when(trainer)
        def _():
            fresh_momentum = momentum_decay * got_hidden[i].astype(wide) + gradient[own_units, :]
            own_hidden[i] = own_hidden[i] - step_size * fresh_momentum

    keep_hidden.start()

    @pl.when(solver)
    def _():
        for j in range(2, len(chunks)):
            update_solver(j)

    @pl.when(trainer)
    def _():
        member = lax.broadcasted_iota(jnp.int32, (batch, batch), 0)
        chosen = jnp.where(member == assignment_ref[...], 1.0, 0.0).astype(narrow)
        for j, c in enumerate(chunks):
            fresh[j].wait_recv()
            own_fields[:, c] = lax.dot_general(
                chosen, got_fields[:, c], (((0,), (0,)), ((), ())), preferred_element_type=wide
            )
            keep_fields[j].start()

    for copy in sends:
        copy.wait_send()

    @pl.when(solver)
    def _():
        for copy in solver_sends:
            copy.wait_send()

    @pl.when(trainer)
    def _():
        for copy in trainer_sends:
            copy.wait_send()

    for copy in keeps:
        copy.wait()


def fused_step(fields, velocity, growth, features, assignment, own_out, own_hidden):
    layer_count, unit_rows, width = own_hidden.shape
    batch, cells = fields.shape
    groups = lax.axis_size("tile") // 4
    rows = batch // lax.axis_size("tile")
    narrow, wide = jnp.bfloat16, jnp.float32
    dma = pltpu.SemaphoreType.DMA
    anywhere = pl.BlockSpec(memory_space=pl.ANY)
    parts, pieces = width // COLUMNS, cells // COLUMNS
    role_slots = layer_count + 3 * pieces + 1 + parts
    return pl.pallas_call(
        functools.partial(train_kernel, groups),
        out_shape=(
            jax.ShapeDtypeStruct(fields.shape, wide),
            jax.ShapeDtypeStruct(own_out.shape, wide),
            jax.ShapeDtypeStruct(own_hidden.shape, wide),
        ),
        in_specs=[anywhere] * 7,
        out_specs=[anywhere] * 3,
        scratch_shapes=[
            pltpu.VMEM((batch, width), narrow),
            pltpu.VMEM((batch, cells), wide),
            pltpu.VMEM((width, cells), wide),
            pltpu.VMEM(own_hidden.shape, wide),
            pltpu.VMEM((1, cells), wide),
            pltpu.VMEM((1, cells), wide),
            pltpu.VMEM((1, batch), jnp.int32),
            pltpu.VMEM((1, LANES), wide),
            pltpu.VMEM((batch, LANES), wide),
            pltpu.VMEM((batch, LANES), wide),
            pltpu.VMEM((width, cells), narrow),
            pltpu.VMEM((width, cells), narrow),
            pltpu.VMEM(own_hidden.shape, narrow),
            pltpu.VMEM((batch, cells), narrow),
            pltpu.VMEM((layer_count, groups, 2, 2, unit_rows, width), narrow),
            pltpu.VMEM((layer_count, batch, width), narrow),
            pltpu.VMEM((layer_count, batch, width), wide),
            pltpu.VMEM((batch, cells), narrow),
            pltpu.VMEM((batch, width), narrow),
            pltpu.VMEM((batch, width), narrow),
            pltpu.VMEM((groups, 2, 2, rows, width), wide),
            pltpu.VMEM((groups, 2, 2, rows, width), narrow),
            pltpu.VMEM((LANES, width), wide),
            pltpu.VMEM((groups, 2, rows, width), wide),
            pltpu.VMEM((groups, rows, width), narrow),
            pltpu.VMEM((groups, rows, width), narrow),
            pltpu.VMEM((groups, rows, width), narrow),
            pltpu.VMEM((groups - 1, rows, width), narrow),
            dma((layer_count, groups - 1)),
            dma((layer_count, groups - 1)),
            dma((layer_count, groups)),
            dma((layer_count, groups)),
            dma((layer_count, 2 * groups)),
            dma((layer_count, 2 * groups)),
            dma((parts, groups + 1)),
            dma((parts, groups + 1)),
            dma((parts, groups + 1)),
            dma((parts, groups + 1)),
            dma((role_slots,)),
            dma((role_slots,)),
            dma((3,)),
            dma((3,)),
            dma((6 + pieces,)),
            dma((2 * pieces + 1,)),
        ],
        compiler_params=pltpu.CompilerParams(
            collective_id=0, has_side_effects=True, vmem_limit_bytes=64000000
        ),
        cost_estimate=pl.CostEstimate(
            flops=60 * batch * width * width, bytes_accessed=40 * batch * width, transcendentals=0
        ),
    )(
        features,
        fields,
        velocity[None, :],
        growth[None, :],
        assignment[None, :],
        own_out,
        own_hidden,
    )


def plain_body(fields_pair, velocity, growth, features, assignment, out_pair, hidden_pair):
    solver_side = lax.axis_index("role") == 0
    own_fields = fields_pair[0]
    own_out = out_pair[0]
    own_hidden = hidden_pair[0]
    stacked = jnp.concatenate([own_fields, velocity[None, :]], axis=0)
    advanced = advance(extended(stacked, "tile", 1, 1), growth)
    grad_out, grad_hidden, other_out, other_hidden, fresh_fields = plain_training(
        features,
        own_hidden.astype(jnp.bfloat16),
        own_out.astype(jnp.bfloat16),
        own_fields,
        own_out,
        own_hidden,
        advanced.astype(jnp.bfloat16),
    )
    grad_out, grad_hidden, other_out, other_hidden = (
        v.astype(jnp.float32) for v in (grad_out, grad_hidden, other_out, other_hidden)
    )
    out_next = jnp.where(
        solver_side,
        momentum_decay * own_out + grad_out,
        own_out - step_size * (momentum_decay * other_out + grad_out),
    )
    hidden_next = jnp.where(
        solver_side,
        momentum_decay * own_hidden + other_hidden,
        own_hidden - step_size * (momentum_decay * other_hidden + grad_hidden),
    )
    next_batch = jnp.take(fresh_fields, assignment, axis=0).astype(jnp.float32)
    fields_next = jnp.where(solver_side, advanced, next_batch)
    return (fields_next[None], out_next[None], hidden_next[None])


def body(fields_pair, velocity, growth, features, assignment, out_pair, hidden_pair):
    tiles = lax.axis_size("tile")
    batch, cells = fields_pair.shape[1:]
    layer_count, unit_rows, width = hidden_pair.shape[1:]
    fits = (
        lax.axis_size("role") == 2
        and tiles % 4 == 0
        and tiles > 4
        and batch % tiles == 0
        and (batch // tiles) % 16 == 0
        and LANES % unit_rows == 0
        and width % COLUMNS == 0
        and cells % COLUMNS == 0
        and cells // COLUMNS == 4
    )
    if not fits:
        return plain_body(
            fields_pair, velocity, growth, features, assignment, out_pair, hidden_pair
        )
    results = fused_step(
        fields_pair[0], velocity, growth, features, assignment, out_pair[0], hidden_pair[0]
    )
    return tuple(result[None] for result in results)


def solution(mesh):
    return jax.shard_map(
        body,
        mesh=mesh,
        in_specs=(
            P("role", None, "tile"),
            P("tile"),
            P("tile"),
            P(),
            P(),
            P("role", None, "tile"),
            P("role", None, "tile", None),
        ),
        out_specs=(P("role", None, "tile"), P("role", None, "tile"), P("role", None, "tile", None)),
        check_vma=False,
    )
```

time: 159 us -> 136 us (0.86)
  other arithmetic: 17.9 us -> 0 us
  starting transfers between devices: 5.5 us -> 0 us
  waiting for transfers between devices: 4.56 us -> 0 us
  Pallas kernels: 125 us -> 128 us
  local copies, waits for them, and re-layouts: 4.87 us -> 6.63 us
    broadcast_in_dim x3 -> x0, other arithmetic: 9.4 us -> none  [body(): return (fields_next[None], out_next[None], hidden_next[None])]
    convert_element_type x3 -> x0, other arithmetic: 6.34 us -> none  [the longest x1 2.39 us: body(): advanced.astype(jnp.bfloat16)]
    unnamed x20 -> x7, local copies, waits for them, and re-layouts: 0.63 us -> 6.63 us
    ppermute x2 -> x0, starting transfers between devices: 5.5 us -> none  [the longest x1 5.5 us: extended(): after = lax.ppermute(leading, axis, down)]
    ppermute x2 -> x0, waiting for transfers between devices: 4.56 us -> none  [the longest x1 4.55 us: extended(): before = lax.ppermute(last, axis, up)]
    gather x1 -> x0, local copies, waits for them, and re-layouts: 4.24 us -> none  [body(): next_batch = jnp.take(fresh_fields, assignment, axis=0).astype(jnp.float32)]
    pallas_call x1, Pallas kernels: 125 us -> 128 us  [fused_step(): pl.pallas_call(functools.partial(train_kernel, groups), out_shape=(jax.Sh...]
  transfers between devices with their start and end apart: 2 -> 0, of which waited for: 1 -> 0; matrix products, arithmetic and copies ran while one was open for 3% -> 0% of each run, Pallas kernels for 0% -> 0%
where the time goes in v1:
time: 136 us; the launch traced here: 135 us
  Pallas kernels  128 us (94%)
  local copies, waits for them, and re-layouts  6.63 us (5%)
    pallas_call x1, Pallas kernels, fused_step(): pl.pallas_call(functools.partial(train_kernel, groups), out_shape=(jax.Sh...  128 us
    unnamed x7, local copies, waits for them, and re-layouts  6.63 us

profile of v1, /device:TPU:0, one launch (start us, length us, event | category | flops | bytes accessed | tf_op | source)
XLA Modules:
  0.0 135.2 jit_solution(16387440084842230654)
XLA Ops:
  0.6 127.9 %shard_map.94 = (f32[512,1024]{1,0:T(8,128)}, f32[1024,1024]{1,0:T(8,128)}, f32[5,64,1024]{2,1,0:T(8,128)}) custom-call(bf16[512,1024]{1,0:T(8,128)(2,1)} %features_hbm.1, f32[512,1024]{1,0:T(8,128)} %bitcast.13, f32[1,1024]{1,0:T(1,128)} %bitcast.15, f32[1,1024]{1,0:T(1,128)} %bitcast.16, s32[1,512]{1,0:T(1,128)} %bitcast.17, f32[1024,1024]{1,0:T(8,128)} %bitcast.12, ...), custom_call_target="tpu_custom_call" | custom-call | flops 32212254720 | bytes 20971520 | tf_op jit(solution)/shard_map/pallas_call | solution.py:642
  128.5 0.0 copy-start
  128.5 3.3 %copy.13 = f32[1,512,1024]{2,1,0:T(8,128)} copy(f32[1,512,1024]{2,1,0:T(8,128)} %bitcast.10) | data formatting | bytes 4194304
  131.9 0.0 copy-done
  131.9 0.0 copy-start.1
  131.9 2.0 %copy.14 = f32[1,1024,1024]{2,1,0:T(8,128)} copy(f32[1,1024,1024]{2,1,0:T(8,128)S(1)} %bitcast.9) | data formatting | bytes 8388608
  133.9 0.2 copy-done.1
  134.1 1.1 copy.15
Async XLA Ops:
  128.5 3.3 %copy-start = (f32[1024,1024]{1,0:T(8,128)S(1)}, f32[1024,1024]{1,0:T(8,128)}, u32[]{:S(2)}) copy-start(f32[1024,1024]{1,0:T(8,128)} %get-tuple-element.7) | copy-start | bytes 12582916
  131.9 2.3 %copy-start.1 = (f32[5,64,1024]{2,1,0:T(8,128)S(1)}, f32[5,64,1024]{2,1,0:T(8,128)}, u32[]{:S(2)}) copy-start(f32[5,64,1024]{2,1,0:T(8,128)} %get-tuple-element.8) | copy-start | bytes 3932164

commit v2 on v1

--- a/solution.py
+++ b/solution.py
@@ -183,7 +183,6 @@
         return (role, z_at * 4 + x_at * 2 + core_at)
 
     z_places = [lax.rem(z + k, groups) for k in range(1, groups)]
-    z_origins = [lax.rem(z + groups - k, groups) for k in range(1, groups)]
     z_peers = [device(place, x, core) for place in z_places]
     x_peer = device(z, 1 - x, core)
     core_peer = device(z, x, 1 - core)
@@ -193,14 +192,14 @@
     far_peer = (role, lax.rem(tile + tiles - 1 + 2 * core, tiles))
     sends, solver_sends, trainer_sends = [], [], []
 
-    def remote(views, semaphores, slot, peer):
+    def remote(views, semaphores, slot, peer, recv_slot=None):
         def build():
             source, target = views()
             return pltpu.make_async_remote_copy(
                 src_ref=source,
                 dst_ref=target,
                 send_sem=semaphores[0].at[slot],
-                recv_sem=semaphores[1].at[slot],
+                recv_sem=semaphores[1].at[slot if recv_slot is None else recv_slot],
                 device_id=peer,
                 device_id_type=pl.DeviceIdType.MESH,
             )
@@ -274,35 +273,92 @@
         remote(views, (edge_send, edge_recv), k, peer) for k, (views, peer) in enumerate(edge_list)
     ]
 
-    z_copies = []
-    x_copies = [[] for _ in range(layer_count)]
-    core_copies = [[] for _ in range(layer_count)]
-
-    def send_x(i, slot, place):
-        view = twice(lambda: weights.at[i, place, x, core])
-        copy = remote(view, (x_send, x_recv), (i, slot), x_peer)
-        x_copies[i].append(start(copy, sends))
+    nearest = [
+        sorted((p for p in range(groups) if p != q), key=lambda p: (abs(p - q), p))
+        for q in range(groups)
+    ]
+
+    def pick(k):
+        place = jnp.int32(nearest[0][k])
+        for q in range(1, groups):
+            place = jnp.where(z == q, nearest[q][k], place)
+        return place
+
+    z_origins = [pick(k) for k in range(groups - 1)]
+    above = device(lax.rem(z + 1, groups), x, core)
+    below = device(lax.rem(z + groups - 1, groups), x, core)
+    spreads, relays = [], []
+
+    def share_of(i, place, x_at):
+        return twice(lambda: weights.at[i, place, x_at, core])
+
+    def hop(i, place, x_at, slot, peer):
+        return remote(
+            share_of(i, place, x_at), (z_send, z_recv), (i, place, x_at, slot), peer, (i, place, x_at)
+        )
+
+    def spread(i, x_at):
+        @pl.when(z < groups - 1)
+        def _():
+            hop(i, z, x_at, 0, above).start()
+
+        @pl.when(z > 0)
+        def _():
+            hop(i, z, x_at, 1, below).start()
+
+        spreads.append((i, x_at))
+
+    def onward(k):
+        rising = z_origins[k] < z
+        return jnp.logical_or(
+            jnp.logical_and(rising, z < groups - 1),
+            jnp.logical_and(jnp.logical_not(rising), z > 0),
+        )
+
+    def relay(i, k, x_at, noted=True):
+        place = z_origins[k]
+        target = jnp.where(place < z, lax.rem(z + 1, groups), lax.rem(z + groups - 1, groups))
+        hop(i, place, x_at, 0, above).wait_recv()
+
+        @pl.when(onward(k))
+        def _():
+            hop(i, place, x_at, 0, device(target, x, core)).start()
+
+        if noted:
+            relays.append((i, k, x_at))
+        if i < last:
+            send_x(i, place)
+        send_core(i, place, x_at)
+
+    def x_copy(i, place):
+        return remote(share_of(i, place, x), (x_send, x_recv), (i, place), x_peer)
+
+    def x_arrival(i, place):
+        return remote(share_of(i, place, 1 - x), (x_send, x_recv), (i, place), x_peer)
+
+    def core_copy(i, place, x_at):
+        return remote(share_of(i, place, x_at), (core_send, core_recv), (i, place, x_at), core_peer)
+
+    def send_x(i, place):
+        x_copy(i, place).start()
 
     def send_core(i, place, x_at):
-        slot = len(core_copies[i])
-        view = twice(lambda: weights.at[i, place, x_at, core])
-        copy = remote(view, (core_send, core_recv), (i, slot), core_peer)
-        core_copies[i].append(start(copy, sends))
+        core_copy(i, place, x_at).start()
+
+    def cross(i, place):
+        x_arrival(i, place).wait_recv()
+        send_core(i, place, 1 - x)
 
     def send_share(i):
         @pl.when(solver)
         def _():
             shares[i].wait_recv()
 
-        view = twice(lambda: weights.at[i, z, x, core])
-        z_copies.append(
-            [
-                start(remote(view, (z_send, z_recv), (i, k), z_peers[k]), sends)
-                for k in range(groups - 1)
-            ]
-        )
-        send_x(i, 0, z)
+        spread(i, x)
+        send_x(i, z)
         send_core(i, z, x)
+
+    share_order = [last] + list(range(last))
 
     def columns_of(j):
         return pl.ds(pl.multiple_of(j * COLUMNS, COLUMNS), COLUMNS)
@@ -351,10 +407,11 @@
         hidden_load.wait()
         for i in range(layer_count):
             weights[i, z, x, core] = own_hidden[i].astype(narrow)
+        for i in share_order:
             start(shares[i], trainer_sends)
 
-    send_share(0)
-    send_share(1)
+    for i in share_order:
+        send_share(i)
 
     for load in small_loads:
         load.wait()
@@ -385,22 +442,50 @@
             inputs[i, :, columns] = (summed * logistic).astype(narrow)
             factors[i, :, columns] = logistic * (1.0 + summed * (1.0 - logistic))
 
-    for i in range(layer_count + 2):
-        if i + 2 < layer_count:
-            send_share(i + 2)
-        if i < layer_count:
-            for k in range(groups - 1):
-                z_copies[i][k].wait_recv()
-                send_x(i, k + 1, z_origins[k])
-                send_core(i, z_origins[k], x)
-        if 1 <= i <= layer_count:
-            for slot, place in enumerate([z] + z_origins):
-                x_copies[i - 1][slot].wait_recv()
-                send_core(i - 1, place, 1 - x)
-        if i >= 2:
-            for copy in core_copies[i - 2]:
-                copy.wait_recv()
-            forward(i - 2)
+    def finish(i):
+        for place in range(groups):
+            for x_at in range(2):
+                arrival = remote(
+                    lambda place=place, x_at=x_at: (weights.at[i, place, x_at, 1 - core],) * 2,
+                    (core_send, core_recv),
+                    (i, place, x_at),
+                    core_peer,
+                )
+                arrival.wait_recv()
+        forward(i)
+
+    relay(last, 0, x)
+    cross(last, z)
+    spread(last, 1 - x)
+    for i in range(last):
+        relay(i, 0, x)
+    relay(last, 0, 1 - x)
+    for i in range(last):
+        cross(i, z)
+    items = [(i, x) for i in range(last)] + [(last, x), (last, 1 - x)]
+    for i, x_at in items:
+        relay(i, 1, x_at)
+    for i in range(last):
+        cross(i, z_origins[0])
+    inner = jnp.logical_and(z > 0, z < groups - 1)
+
+    @pl.when(inner)
+    def _():
+        for i, x_at in items:
+            relay(i, 2, x_at)
+
+    for step, (i, x_at) in enumerate(items):
+
+        @pl.when(jnp.logical_not(inner))
+        def _():
+            relay(i, 2, x_at, False)
+
+        if step < last:
+            cross(i, z_origins[1])
+        if step >= 2:
+            cross(step - 2, z_origins[2])
+            finish(step - 2)
+    finish(last)
 
     def update_out(j, decay, rate, other):
         c = chunks[j]
@@ -614,6 +699,28 @@
 
     for copy in sends:
         copy.wait_send()
+    for i in range(layer_count):
+        for place in range(groups):
+            if i < last:
+                x_copy(i, place).wait_send()
+            for x_at in range(2):
+                core_copy(i, place, x_at).wait_send()
+    x_copy(last, z).wait_send()
+    for i, x_at in spreads:
+
+        @pl.when(z < groups - 1)
+        def _():
+            hop(i, z, x_at, 0, above).wait_send()
+
+        @pl.when(z > 0)
+        def _():
+            hop(i, z, x_at, 1, below).wait_send()
+
+    for i, k, x_at in relays:
+
+        @pl.when(onward(k))
+        def _():
+            hop(i, z_origins[k], x_at, 0, above).wait_send()
 
     @pl.when(solver)
     def _():
@@ -677,12 +784,12 @@
             pltpu.VMEM((groups, rows, width), narrow),
             pltpu.VMEM((groups, rows, width), narrow),
             pltpu.VMEM((groups - 1, rows, width), narrow),
-            dma((layer_count, groups - 1)),
-            dma((layer_count, groups - 1)),
+            dma((layer_count, groups, 2, 2)),
+            dma((layer_count, groups, 2)),
             dma((layer_count, groups)),
             dma((layer_count, groups)),
-            dma((layer_count, 2 * groups)),
-            dma((layer_count, 2 * groups)),
+            dma((layer_count, groups, 2)),
+            dma((layer_count, groups, 2)),
             dma((parts, groups + 1)),
             dma((parts, groups + 1)),
             dma((parts, groups + 1)),
@@ -751,8 +858,8 @@
     layer_count, unit_rows, width = hidden_pair.shape[1:]
     fits = (
         lax.axis_size("role") == 2
-        and tiles % 4 == 0
-        and tiles > 4
+        and tiles == 16
+        and layer_count > 2
         and batch % tiles == 0
         and (batch // tiles) % 16 == 0
         and LANES % unit_rows == 0

time: 136 us -> 123 us (0.904)
  Pallas kernels: 128 us -> 115 us
    pallas_call x1, Pallas kernels: 128 us -> 115 us  [fused_step(): pl.pallas_call(functools.partial(train_kernel, groups), out_shape=(jax.Sh...]
where the time goes in v2:
time: 123 us; the launch traced here: 122 us
  Pallas kernels  115 us (93%)
  local copies, waits for them, and re-layouts  6.63 us (5%)
    pallas_call x1, Pallas kernels, fused_step(): pl.pallas_call(functools.partial(train_kernel, groups), out_shape=(jax.Sh...  115 us
    unnamed x7, local copies, waits for them, and re-layouts  6.63 us

profile of v2, /device:TPU:0, one launch (start us, length us, event | category | flops | bytes accessed | tf_op | source)
XLA Modules:
  0.0 122.1 jit_solution(6899068590988185871)
XLA Ops:
  0.6 114.8 %shard_map.94 = (f32[512,1024]{1,0:T(8,128)}, f32[1024,1024]{1,0:T(8,128)}, f32[5,64,1024]{2,1,0:T(8,128)}) custom-call(bf16[512,1024]{1,0:T(8,128)(2,1)} %features_hbm.1, f32[512,1024]{1,0:T(8,128)} %bitcast.13, f32[1,1024]{1,0:T(1,128)} %bitcast.15, f32[1,1024]{1,0:T(1,128)} %bitcast.16, s32[1,512]{1,0:T(1,128)} %bitcast.17, f32[1024,1024]{1,0:T(8,128)} %bitcast.12, ...), custom_call_target="tpu_custom_call" | custom-call | flops 32212254720 | bytes 20971520 | tf_op jit(solution)/shard_map/pallas_call | solution.py:749
  115.4 0.0 copy-start
  115.4 3.3 %copy.13 = f32[1,512,1024]{2,1,0:T(8,128)} copy(f32[1,512,1024]{2,1,0:T(8,128)} %bitcast.10) | data formatting | bytes 4194304
  118.8 0.0 copy-done
  118.8 0.0 copy-start.1
  118.8 2.0 %copy.14 = f32[1,1024,1024]{2,1,0:T(8,128)} copy(f32[1,1024,1024]{2,1,0:T(8,128)S(1)} %bitcast.9) | data formatting | bytes 8388608
  120.8 0.2 copy-done.1
  121.0 1.1 copy.15
Async XLA Ops:
  115.4 3.3 %copy-start = (f32[1024,1024]{1,0:T(8,128)S(1)}, f32[1024,1024]{1,0:T(8,128)}, u32[]{:S(2)}) copy-start(f32[1024,1024]{1,0:T(8,128)} %get-tuple-element.7) | copy-start | bytes 12582916
  118.8 2.3 %copy-start.1 = (f32[5,64,1024]{2,1,0:T(8,128)S(1)}, f32[5,64,1024]{2,1,0:T(8,128)}, u32[]{:S(2)}) copy-start(f32[5,64,1024]{2,1,0:T(8,128)} %get-tuple-element.8) | copy-start | bytes 3932164

commit v3 on v2

--- a/solution.py
+++ b/solution.py
@@ -117,13 +117,10 @@
     assignment_hbm,
     out_hbm,
     hidden_hbm,
-    fields_next,
-    out_next,
-    hidden_next,
-    features_ref,
     own_fields,
     own_out,
     own_hidden,
+    features_ref,
     velocity_ref,
     growth_ref,
     assignment_ref,
@@ -136,13 +133,16 @@
     got_fields,
     weights,
     inputs,
+    top,
     factors,
     residual,
     slope_even,
     slope_odd,
     partial,
+    core_away,
     slope,
     gradient,
+    got_gradient,
     core_sum,
     x_away,
     x_sum,
@@ -160,14 +160,16 @@
     slope_recv,
     role_send,
     role_recv,
+    pair_send,
+    pair_recv,
     edge_send,
     edge_recv,
     local_sem,
-    keep_sem,
 ):
     layer_count, unit_rows, width = hidden_hbm.shape
     batch, cells = fields_hbm.shape
-    rows = partial.shape[3]
+    rows = partial.shape[2]
+    half = batch // 2
     narrow, wide = jnp.bfloat16, jnp.float32
     tiles = groups * 4
     last = layer_count - 1
@@ -230,19 +232,14 @@
 
     chunks = [pl.ds(j * COLUMNS, COLUMNS) for j in range(cells // COLUMNS)]
     parts = [pl.ds(j * COLUMNS, COLUMNS) for j in range(width // COLUMNS)]
+    pieces = [pl.ds(j * LANES, LANES) for j in range(width // LANES)]
+    per_part = COLUMNS // LANES
     shares = [across(lambda i=i: weights.at[i, z, x, core]) for i in range(layer_count)]
     momenta = [across(lambda c=c: got_out.at[:, c]) for c in chunks]
     hidden_momentum = across(lambda: got_hidden)
     fresh = [across(lambda c=c: got_fields.at[:, c]) for c in chunks]
-    residuals = [across(lambda c=c: residual.at[:, c]) for c in chunks]
-    slope_shares = [across(lambda c=c: slope.at[z, x, core, :, c]) for c in parts]
-
-    kept = [lambda c=c: (own_fields.at[:, c], fields_next.at[:, c]) for c in chunks]
-    kept += [lambda c=c: (own_out.at[:, c], out_next.at[:, c]) for c in chunks]
-    kept += [lambda: (own_hidden, hidden_next)]
-    keeps = [local(views, keep_sem, k) for k, views in enumerate(kept)]
-    keep_fields, keep_out = keeps[: len(chunks)], keeps[len(chunks) : -1]
-    keep_hidden = keeps[-1]
+    residuals = [across(lambda c=c: residual.at[:, :, :, :, c]) for c in chunks]
+    slope_shares = [across(lambda c=c: slope.at[z, x, :, c]) for c in pieces]
 
     pairs = [lambda: (hidden_hbm, own_hidden)]
     pairs += [lambda c=c: (out_hbm.at[:, c], own_out.at[:, c]) for c in chunks]
@@ -421,9 +418,8 @@
         for copy in edges:
             copy.wait_recv()
         advance()
-        for copy, written in zip(fresh, keep_fields):
+        for copy in fresh:
             start(copy, solver_sends)
-            written.start()
 
     @pl.when(trainer)
     def _():
@@ -431,16 +427,42 @@
             load.wait()
             out_ref[:, c] = own_out[:, c].astype(narrow)
 
+    pair_slots = [0]
+
+    def beside(views):
+        slot = pair_slots[0]
+        pair_slots[0] += 1
+        return remote(views, (pair_send, pair_recv), slot, core_peer)
+
+    tops = [beside(twice(lambda c=c: top.at[:, :, core, :, c])) for c in parts]
+    own_units = pl.ds(pl.multiple_of(core * unit_rows, unit_rows), unit_rows)
+    other_units = pl.ds(pl.multiple_of((1 - core) * unit_rows, unit_rows), unit_rows)
+    halves = [
+        beside(lambda i=i: (gradient.at[i, other_units, :], got_gradient.at[i]))
+        for i in range(layer_count)
+    ]
+
+    def forward_columns(i, columns):
+        block = weights[i, :, :, :, :, columns].reshape(width, COLUMNS)
+        activation = features_ref[:, :, core] if i == 0 else inputs[i - 1]
+        summed = jnp.dot(activation.reshape(half, width), block, preferred_element_type=wide)
+        logistic = jax.nn.sigmoid(summed)
+        result = (summed * logistic).astype(narrow).reshape(groups, 2, rows, COLUMNS)
+        factor = logistic * (1.0 + summed * (1.0 - logistic))
+        factors[i, :, :, :, columns] = factor.reshape(groups, 2, rows, COLUMNS)
+        return result
+
     def forward(i):
-        @pl.loop(0, width // COLUMNS)
-        def _(j):
-            columns = columns_of(j)
-            block = weights[i, :, :, :, :, columns].reshape(width, COLUMNS)
-            activation = features_ref[...] if i == 0 else inputs[i - 1]
-            summed = jnp.dot(activation, block, preferred_element_type=wide)
-            logistic = jax.nn.sigmoid(summed)
-            inputs[i, :, columns] = (summed * logistic).astype(narrow)
-            factors[i, :, columns] = logistic * (1.0 + summed * (1.0 - logistic))
+        if i == last:
+            for c, copy in zip(parts, tops):
+                top[:, :, core, :, c] = forward_columns(i, c)
+                start(copy, sends)
+        else:
+
+            @pl.loop(0, width // COLUMNS)
+            def _(j):
+                columns = columns_of(j)
+                inputs[i, :, :, :, columns] = forward_columns(i, columns)
 
     def finish(i):
         for place in range(groups):
@@ -494,8 +516,8 @@
         def _(k):
             units = columns_of(k)
             grad = lax.dot_general(
-                inputs[last, :, units],
-                residual[:, c],
+                top[:, :, :, :, units].reshape(batch, COLUMNS),
+                residual[:, :, :, :, c].reshape(batch, COLUMNS),
                 (((0,), (0,)), ((), ())),
                 preferred_element_type=wide,
             )
@@ -505,8 +527,6 @@
                 fresh_momentum = decay * other[units, c].astype(wide) + grad
                 own_out[units, c] = own_out[units, c] - rate * fresh_momentum
 
-        keep_out[j].start()
-
     def update_solver(j):
         residuals[j].wait_recv()
         update_out(j, momentum_decay, None, None)
@@ -515,63 +535,71 @@
         momenta[j].wait_recv()
         update_out(j, momentum_decay, step_size, got_out)
 
-    core_sums, x_sums, z_sums, z_slopes, x_slopes, core_slopes = [], [], [], [], [], []
+    x_sums, z_sums = [], []
 
     def send_sum(views, j, slot, peer):
         return start(remote(views, (sum_send, sum_recv), (j, slot), peer), trainer_sends)
 
+    core_sums = [
+        remote(
+            lambda c=c: (core_away.at[:, :, :, c], core_sum.at[:, :, :, c]),
+            (sum_send, sum_recv),
+            (j, 0),
+            core_peer,
+        )
+        for j, c in enumerate(parts)
+    ]
+    targets = own_fields.reshape(groups, 2, 2, rows, cells)
+
+    def residual_columns(side, c):
+        rows_of = top[:, :, side].reshape(half, width)
+        predicted = jnp.dot(rows_of, out_ref[:, c], preferred_element_type=wide)
+        wanted = targets[:, :, side, :, c].reshape(half, COLUMNS)
+        kept = ((predicted - wanted) / batch).astype(narrow)
+        residual[:, :, side, :, c] = kept.reshape(groups, 2, rows, COLUMNS)
+
+    def upstream_columns(side, c):
+        return lax.dot_general(
+            residual[:, :, side].reshape(half, cells),
+            out_ref[c, :],
+            (((1,), (1,)), ((), ())),
+            preferred_element_type=wide,
+        ).reshape(groups, 2, rows, COLUMNS)
+
     @pl.when(trainer)
     def _():
+        for c in chunks:
+            residual_columns(core, c)
+        for copy in tops:
+            copy.wait_recv()
         for j, c in enumerate(chunks):
-            predicted = jnp.dot(inputs[last], out_ref[:, c], preferred_element_type=wide)
-            residual[:, c] = ((predicted - own_fields[:, c]) / batch).astype(narrow)
-            if j + 1 < len(chunks):
+            residual_columns(1 - core, c)
+            if j < 2:
                 start(residuals[j], trainer_sends)
-        for j, columns in enumerate(parts):
-            part = lax.dot_general(
-                residual[...],
-                out_ref[columns, :],
-                (((1,), (1,)), ((), ())),
-                preferred_element_type=wide,
-            )
-            partial[:, :, :, :, columns] = part.reshape(groups, 2, 2, rows, COLUMNS)
-            core_sums.append(
-                send_sum(
-                    lambda columns=columns: (
-                        partial.at[:, :, 1 - core, :, columns],
-                        core_sum.at[:, :, :, columns],
-                    ),
-                    j,
-                    0,
-                    core_peer,
+        for c, copy in zip(parts, core_sums):
+            core_away[:, :, :, c] = upstream_columns(1 - core, c)
+            start(copy, trainer_sends)
+        for j, c in enumerate(parts):
+            partial[:, :, :, c] = upstream_columns(core, c)
+            core_sums[j].wait_recv()
+            x_away[:, :, c] = (partial[:, 1 - x, :, c] + core_sum[:, 1 - x, :, c]).astype(narrow)
+            for q in range(j * per_part, (j + 1) * per_part):
+                x_sums.append(
+                    send_sum(
+                        lambda c=pieces[q]: (x_away.at[:, :, c], x_sum.at[:, :, c]), q, 1, x_peer
+                    )
                 )
-            )
-        for j, columns in enumerate(parts):
-            core_sums[j].wait_recv()
-            away = partial[:, 1 - x, core, :, columns] + core_sum[:, 1 - x, :, columns]
-            x_away[:, :, columns] = away.astype(narrow)
-            x_sums.append(
-                send_sum(
-                    lambda columns=columns: (x_away.at[:, :, columns], x_sum.at[:, :, columns]),
-                    j,
-                    1,
-                    x_peer,
-                )
-            )
         update_trainer(0)
-        for j, columns in enumerate(parts):
-            near = partial[:, x, core, :, columns] + core_sum[:, x, :, columns]
+        for j, c in enumerate(pieces):
+            near = partial[:, x, :, c] + core_sum[:, x, :, c]
             x_sums[j].wait_recv()
-            near = near + x_sum[:, :, columns].astype(wide)
-            partial[:, x, core, :, columns] = near
-            z_away[:, :, columns] = near.astype(narrow)
+            near = near + x_sum[:, :, c].astype(wide)
+            partial[:, x, :, c] = near
+            z_away[:, :, c] = near.astype(narrow)
             z_sums.append(
                 [
                     send_sum(
-                        lambda columns=columns, k=k: (
-                            z_away.at[z_places[k], :, columns],
-                            z_sum.at[k, :, columns],
-                        ),
+                        lambda c=c, k=k: (z_away.at[z_places[k], :, c], z_sum.at[k, :, c]),
                         j,
                         2 + k,
                         z_peers[k],
@@ -583,65 +611,69 @@
 
     @pl.when(solver)
     def _():
+        for copy in tops:
+            copy.wait_recv()
         update_solver(0)
         update_solver(1)
 
-    own_rows = pl.ds(pl.multiple_of(tile * rows, rows), rows)
-
     def send_slope(view, j, slot, peer):
         return start(remote(twice(view), (slope_send, slope_recv), (j, slot), peer), sends)
 
-    for j, columns in enumerate(parts):
+    z_slopes, x_slopes = [], []
+    for j, c in enumerate(pieces):
 
         @pl.when(trainer)
         def _():
-            upstream = partial[z, x, core, :, columns]
+            upstream = partial[z, x, :, c]
             for k in range(groups - 1):
                 z_sums[j][k].wait_recv()
-                upstream = upstream + z_sum[k, :, columns].astype(wide)
-            slope[z, x, core, :, columns] = (upstream * factors[last, own_rows, columns]).astype(
-                narrow
-            )
+                upstream = upstream + z_sum[k, :, c].astype(wide)
+            slope[z, x, :, c] = (upstream * factors[last, z, x, :, c]).astype(narrow)
             start(slope_shares[j], trainer_sends)
 
         @pl.when(solver)
         def _():
             slope_shares[j].wait_recv()
 
-        view = lambda columns=columns: slope.at[z, x, core, :, columns]
+        view = lambda c=c: slope.at[z, x, :, c]
         z_slopes.append([send_slope(view, j, k, z_peers[k]) for k in range(groups - 1)])
 
     @pl.when(trainer)
     def _():
-        start(residuals[-1], trainer_sends)
+        for copy in residuals[2:]:
+            start(copy, trainer_sends)
         update_trainer(2)
 
-    for j, columns in enumerate(parts):
+    for j, c in enumerate(pieces):
         for copy in z_slopes[j]:
             copy.wait_recv()
-        x_slopes.append(send_slope(
-            lambda columns=columns: slope.at[:, x, core, :, columns], j, groups - 1, x_peer
-        ))
-    for j, columns in enumerate(parts):
-        x_slopes[j].wait_recv()
-        core_slopes.append(send_slope(
-            lambda columns=columns: slope.at[:, :, core, :, columns], j, groups, core_peer
-        ))
+        x_slopes.append(send_slope(lambda c=c: slope.at[:, x, :, c], j, groups - 1, x_peer))
 
     @pl.when(trainer)
     def _():
         update_trainer(3)
         hidden_momentum.wait_recv()
 
-    for copy in core_slopes:
+    for copy in x_slopes:
         copy.wait_recv()
 
-    per_block = LANES // unit_rows
-    first_lane = pl.multiple_of((tile // per_block) * LANES, LANES)
-    unit_first = pl.multiple_of(lax.rem(tile, per_block) * unit_rows, unit_rows)
-    slopes = [slope.reshape(batch, width), slope_even, slope_odd]
+    first_lane = pl.multiple_of((tile // 2) * LANES, LANES)
+
+    def update_hidden(i):
+        halves[i].wait_recv()
+        total = gradient[i, own_units, :] + got_gradient[i]
+
+        @pl.when(solver)
+        def _():
+            own_hidden[i] = momentum_decay * own_hidden[i] + total
+
+        @pl.when(trainer)
+        def _():
+            fresh_momentum = momentum_decay * got_hidden[i].astype(wide) + total
+            own_hidden[i] = own_hidden[i] - step_size * fresh_momentum
+
+    slopes = [slope, slope_even, slope_odd]
     for step, i in enumerate(reversed(range(layer_count))):
-        source = features_ref if i == 0 else inputs.at[i - 1]
         this_slope = slopes[0] if step == 0 else slopes[1 + step % 2]
         next_slope = slopes[1 + (step + 1) % 2]
         if i > 0:
@@ -651,35 +683,32 @@
                 columns = columns_of(j)
                 block = weights.at[i].reshape(width, width)[columns, :]
                 back = lax.dot_general(
-                    this_slope[...],
+                    this_slope[...].reshape(half, width),
                     block,
                     (((1,), (1,)), ((), ())),
                     preferred_element_type=wide,
                 )
-                next_slope[:, columns] = (back * factors[i - 1, :, columns]).astype(narrow)
+                factor = factors[i - 1, :, :, :, columns].reshape(half, COLUMNS)
+                next_slope[:, :, :, columns] = (
+                    (back * factor).astype(narrow).reshape(groups, 2, rows, COLUMNS)
+                )
+
+        lanes = pl.ds(first_lane, LANES)
+        own_inputs = features_ref[:, :, core, :, lanes] if i == 0 else inputs[i - 1, :, :, :, lanes]
 
         @pl.loop(0, width // COLUMNS)
         def _(j):
             columns = columns_of(j)
-            gradient[:, columns] = lax.dot_general(
-                source[:, pl.ds(first_lane, LANES)],
-                this_slope[:, columns],
+            gradient[i, :, columns] = lax.dot_general(
+                own_inputs.reshape(half, LANES),
+                this_slope[:, :, :, columns].reshape(half, COLUMNS),
                 (((0,), (0,)), ((), ())),
                 preferred_element_type=wide,
             )
 
-        own_units = pl.ds(unit_first, unit_rows)
-
-        @pl.when(solver)
-        def _():
-            own_hidden[i] = momentum_decay * own_hidden[i] + gradient[own_units, :]
-
-        @pl.when(trainer)
-        def _():
-            fresh_momentum = momentum_decay * got_hidden[i].astype(wide) + gradient[own_units, :]
-            own_hidden[i] = own_hidden[i] - step_size * fresh_momentum
-
-    keep_hidden.start()
+        start(halves[i], sends)
+        if i < last:
+            update_hidden(i + 1)
 
     @pl.when(solver)
     def _():
@@ -695,7 +724,8 @@
             own_fields[:, c] = lax.dot_general(
                 chosen, got_fields[:, c], (((0,), (0,)), ((), ())), preferred_element_type=wide
             )
-            keep_fields[j].start()
+
+    update_hidden(0)
 
     for copy in sends:
         copy.wait_send()
@@ -732,9 +762,6 @@
         for copy in trainer_sends:
             copy.wait_send()
 
-    for copy in keeps:
-        copy.wait()
-
 
 def fused_step(fields, velocity, growth, features, assignment, own_out, own_hidden):
     layer_count, unit_rows, width = own_hidden.shape
@@ -743,9 +770,11 @@
     rows = batch // lax.axis_size("tile")
     narrow, wide = jnp.bfloat16, jnp.float32
     dma = pltpu.SemaphoreType.DMA
-    anywhere = pl.BlockSpec(memory_space=pl.ANY)
+    anywhere = pl.BlockSpec(memory_space=pltpu.HBM)
     parts, pieces = width // COLUMNS, cells // COLUMNS
-    role_slots = layer_count + 3 * pieces + 1 + parts
+    splits = width // LANES
+    role_slots = layer_count + 3 * pieces + 1 + splits
+    split = (groups, 2, 2, rows, width)
     return pl.pallas_call(
         functools.partial(train_kernel, groups),
         out_shape=(
@@ -754,12 +783,9 @@
             jax.ShapeDtypeStruct(own_hidden.shape, wide),
         ),
         in_specs=[anywhere] * 7,
-        out_specs=[anywhere] * 3,
+        out_specs=[pl.BlockSpec(memory_space=pltpu.VMEM)] * 3,
         scratch_shapes=[
-            pltpu.VMEM((batch, width), narrow),
-            pltpu.VMEM((batch, cells), wide),
-            pltpu.VMEM((width, cells), wide),
-            pltpu.VMEM(own_hidden.shape, wide),
+            pltpu.VMEM(split, narrow),
             pltpu.VMEM((1, cells), wide),
             pltpu.VMEM((1, cells), wide),
             pltpu.VMEM((1, batch), jnp.int32),
@@ -771,14 +797,17 @@
             pltpu.VMEM(own_hidden.shape, narrow),
             pltpu.VMEM((batch, cells), narrow),
             pltpu.VMEM((layer_count, groups, 2, 2, unit_rows, width), narrow),
-            pltpu.VMEM((layer_count, batch, width), narrow),
-            pltpu.VMEM((layer_count, batch, width), wide),
-            pltpu.VMEM((batch, cells), narrow),
-            pltpu.VMEM((batch, width), narrow),
-            pltpu.VMEM((batch, width), narrow),
-            pltpu.VMEM((groups, 2, 2, rows, width), wide),
-            pltpu.VMEM((groups, 2, 2, rows, width), narrow),
-            pltpu.VMEM((LANES, width), wide),
+            pltpu.VMEM((layer_count - 1, groups, 2, rows, width), narrow),
+            pltpu.VMEM(split, narrow),
+            pltpu.VMEM((layer_count, groups, 2, rows, width), wide),
+            pltpu.VMEM((groups, 2, 2, rows, cells), narrow),
+            pltpu.VMEM((groups, 2, rows, width), narrow),
+            pltpu.VMEM((groups, 2, rows, width), narrow),
+            pltpu.VMEM((groups, 2, rows, width), wide),
+            pltpu.VMEM((groups, 2, rows, width), wide),
+            pltpu.VMEM((groups, 2, rows, width), narrow),
+            pltpu.VMEM((layer_count, LANES, width), wide),
+            pltpu.VMEM(own_hidden.shape, wide),
             pltpu.VMEM((groups, 2, rows, width), wide),
             pltpu.VMEM((groups, rows, width), narrow),
             pltpu.VMEM((groups, rows, width), narrow),
@@ -790,31 +819,37 @@
             dma((layer_count, groups)),
             dma((layer_count, groups, 2)),
             dma((layer_count, groups, 2)),
-            dma((parts, groups + 1)),
-            dma((parts, groups + 1)),
-            dma((parts, groups + 1)),
-            dma((parts, groups + 1)),
+            dma((splits, groups + 1)),
+            dma((splits, groups + 1)),
+            dma((splits, groups)),
+            dma((splits, groups)),
             dma((role_slots,)),
             dma((role_slots,)),
+            dma((parts + layer_count,)),
+            dma((parts + layer_count,)),
             dma((3,)),
             dma((3,)),
             dma((6 + pieces,)),
-            dma((2 * pieces + 1,)),
         ],
         compiler_params=pltpu.CompilerParams(
-            collective_id=0, has_side_effects=True, vmem_limit_bytes=64000000
+            collective_id=0, has_side_effects=True, vmem_limit_bytes=46000000
         ),
         cost_estimate=pl.CostEstimate(
             flops=60 * batch * width * width, bytes_accessed=40 * batch * width, transcendentals=0
         ),
     )(
-        features,
-        fields,
-        velocity[None, :],
-        growth[None, :],
-        assignment[None, :],
-        own_out,
-        own_hidden,
+        *(
+            pltpu.with_memory_space_constraint(value, pltpu.HBM)
+            for value in (
+                features.reshape(split),
+                fields,
+                velocity[None, :],
+                growth[None, :],
+                assignment[None, :],
+                own_out,
+                own_hidden,
+            )
+        )
     )
 
 
@@ -862,7 +897,7 @@
         and layer_count > 2
         and batch % tiles == 0
         and (batch // tiles) % 16 == 0
-        and LANES % unit_rows == 0
+        and LANES == 2 * unit_rows
         and width % COLUMNS == 0
         and cells % COLUMNS == 0
         and cells // COLUMNS == 4

time: 123 us -> 112 us (0.911)
  Pallas kernels: 115 us -> 107 us
  local copies, waits for them, and re-layouts: 6.63 us -> 4.39 us
    pallas_call x1, Pallas kernels: 115 us -> 107 us  [fused_step(): pl.pallas_call(functools.partial(train_kernel, groups), out_shape=(jax.Sh...]
    unnamed x7 -> x3, local copies, waits for them, and re-layouts: 6.63 us -> 4.39 us
where the time goes in v3:
time: 112 us
  Pallas kernels  107 us (96%)
  local copies, waits for them, and re-layouts  4.39 us (4%)
    pallas_call x1, Pallas kernels, fused_step(): pl.pallas_call(functools.partial(train_kernel, groups), out_shape=(jax.Sh...  107 us
    unnamed x3, local copies, waits for them, and re-layouts  4.39 us

profile of v3, /device:TPU:0, one launch (start us, length us, event | category | flops | bytes accessed | tf_op | source)
XLA Modules:
  0.0 111.5 jit_solution(14462620444971993340)
XLA Ops:
  0.6 106.5 %shard_map.94 = (f32[512,1024]{1,0:T(8,128)S(1)}, f32[1024,1024]{1,0:T(8,128)S(1)}, f32[5,64,1024]{2,1,0:T(8,128)S(1)}) custom-call(bf16[4,2,2,32,1024]{4,3,2,1,0:T(8,128)(2,1)} %bitcast.16, f32[512,1024]{1,0:T(8,128)} %bitcast.14, f32[1,1024]{1,0:T(1,128)} %bitcast.17, f32[1,1024]{1,0:T(1,128)} %bitcast.18, s32[1,512]{1,0:T(1,128)} %bitcast.19, ...), custom_call_target="tpu_custom_call" | custom-call | flops 32212254720 | bytes 20971520 | tf_op jit(solution)/shard_map/pallas_call | solution.py:778
  107.2 1.3 %copy.13 = f32[1,512,1024]{2,1,0:T(8,128)} copy(f32[1,512,1024]{2,1,0:T(8,128)S(1)} %bitcast.11) | data formatting | bytes 4194304
  108.5 2.0 %copy.14 = f32[1,1024,1024]{2,1,0:T(8,128)} copy(f32[1,1024,1024]{2,1,0:T(8,128)S(1)} %bitcast.10) | data formatting | bytes 8388608
  110.5 1.1 copy.15

commit v4 on v3

--- a/solution.py
+++ b/solution.py
@@ -127,6 +127,7 @@
     left_velocity,
     left_edge,
     right_edge,
+    lent_fields,
     out_ref,
     got_out,
     got_hidden,
@@ -192,16 +193,15 @@
     right_peer = (role, lax.rem(tile + 1, tiles))
     left_peer = (role, lax.rem(tile + tiles - 1, tiles))
     far_peer = (role, lax.rem(tile + tiles - 1 + 2 * core, tiles))
-    sends, solver_sends, trainer_sends = [], [], []
-
-    def remote(views, semaphores, slot, peer, recv_slot=None):
+
+    def remote(views, sent, arrived, peer):
         def build():
             source, target = views()
             return pltpu.make_async_remote_copy(
                 src_ref=source,
                 dst_ref=target,
-                send_sem=semaphores[0].at[slot],
-                recv_sem=semaphores[1].at[slot if recv_slot is None else recv_slot],
+                send_sem=sent[0].at[sent[1]],
+                recv_sem=arrived[0].at[arrived[1]],
                 device_id=peer,
                 device_id_type=pl.DeviceIdType.MESH,
             )
@@ -218,28 +218,37 @@
     def twice(view):
         return lambda: (view(),) * 2
 
-    def start(copy, among):
-        copy.start()
-        among.append(copy)
-        return copy
-
-    role_slots = [0]
-
-    def across(view):
-        slot = role_slots[0]
-        role_slots[0] += 1
-        return remote(twice(view), (role_send, role_recv), slot, role_peer)
+    def across(view, kind, slot):
+        return remote(twice(view), (role_send, kind), (role_recv, slot), role_peer)
 
     chunks = [pl.ds(j * COLUMNS, COLUMNS) for j in range(cells // COLUMNS)]
     parts = [pl.ds(j * COLUMNS, COLUMNS) for j in range(width // COLUMNS)]
     pieces = [pl.ds(j * LANES, LANES) for j in range(width // LANES)]
     per_part = COLUMNS // LANES
-    shares = [across(lambda i=i: weights.at[i, z, x, core]) for i in range(layer_count)]
-    momenta = [across(lambda c=c: got_out.at[:, c]) for c in chunks]
-    hidden_momentum = across(lambda: got_hidden)
-    fresh = [across(lambda c=c: got_fields.at[:, c]) for c in chunks]
-    residuals = [across(lambda c=c: residual.at[:, :, :, :, c]) for c in chunks]
-    slope_shares = [across(lambda c=c: slope.at[z, x, :, c]) for c in pieces]
+    count = len(chunks)
+    lent = count // 2
+    lent_cells = pl.ds(lent * COLUMNS, (count - lent) * COLUMNS)
+    momenta = [across(lambda c=c: got_out.at[:, c], 0, j) for j, c in enumerate(chunks)]
+    hidden_momentum = across(lambda: got_hidden, 1, count)
+    fresh = [
+        across(lambda c=c: got_fields.at[:, c], 2, count + 1 + j) for j, c in enumerate(chunks)
+    ]
+    shares = [across(lambda i=i: weights.at[i, z, x, core], 0, i) for i in range(layer_count)]
+    lent_out = across(lambda: out_ref.at[:, lent_cells], 1, layer_count)
+    lent_target = remote(
+        lambda: (own_fields.at[:, lent_cells], lent_fields),
+        (role_send, 2),
+        (role_recv, layer_count + 1),
+        role_peer,
+    )
+    residuals = [
+        across(lambda c=c: residual.at[:, :, :, :, c], 3, layer_count + 2 + j)
+        for j, c in enumerate(chunks[:lent])
+    ]
+    slope_shares = [
+        across(lambda c=c: slope.at[z, x, :, c], 4, layer_count + 2 + lent + j)
+        for j, c in enumerate(pieces)
+    ]
 
     pairs = [lambda: (hidden_hbm, own_hidden)]
     pairs += [lambda c=c: (out_hbm.at[:, c], own_out.at[:, c]) for c in chunks]
@@ -267,7 +276,8 @@
         (lambda: (fields_hbm.at[:, pl.ds(0, LANES)], right_edge), left_peer),
     ]
     edges = [
-        remote(views, (edge_send, edge_recv), k, peer) for k, (views, peer) in enumerate(edge_list)
+        remote(views, (edge_send, k), (edge_recv, k), peer)
+        for k, (views, peer) in enumerate(edge_list)
     ]
 
     nearest = [
@@ -282,28 +292,31 @@
         return place
 
     z_origins = [pick(k) for k in range(groups - 1)]
-    above = device(lax.rem(z + 1, groups), x, core)
-    below = device(lax.rem(z + groups - 1, groups), x, core)
-    spreads, relays = [], []
+    inner = jnp.logical_and(z > 0, z < groups - 1)
 
     def share_of(i, place, x_at):
         return twice(lambda: weights.at[i, place, x_at, core])
 
-    def hop(i, place, x_at, slot, peer):
+    def hop(i, place, item, kind, target):
+        rank = jnp.where(place > target, place - 1, place)
+        x_at = 1 - x if item == layer_count else x
         return remote(
-            share_of(i, place, x_at), (z_send, z_recv), (i, place, x_at, slot), peer, (i, place, x_at)
+            share_of(i, place, x_at),
+            (z_send, kind + 2 * (item // layer_count)),
+            (z_recv, (item, rank)),
+            device(target, x, core),
         )
 
-    def spread(i, x_at):
+    def spread(item):
+        i = min(item, last)
+
         @pl.when(z < groups - 1)
         def _():
-            hop(i, z, x_at, 0, above).start()
+            hop(i, z, item, 0, lax.rem(z + 1, groups)).start()
 
         @pl.when(z > 0)
         def _():
-            hop(i, z, x_at, 1, below).start()
-
-        spreads.append((i, x_at))
+            hop(i, z, item, jnp.where(z == groups - 1, 0, 1), lax.rem(z + groups - 1, groups)).start()
 
     def onward(k):
         rising = z_origins[k] < z
@@ -312,47 +325,50 @@
             jnp.logical_and(jnp.logical_not(rising), z > 0),
         )
 
-    def relay(i, k, x_at, noted=True):
+    def relay(item, k):
+        i = min(item, last)
         place = z_origins[k]
-        target = jnp.where(place < z, lax.rem(z + 1, groups), lax.rem(z + groups - 1, groups))
-        hop(i, place, x_at, 0, above).wait_recv()
+        hop(i, place, item, 1, z).wait_recv()
 
         @pl.when(onward(k))
         def _():
-            hop(i, place, x_at, 0, device(target, x, core)).start()
-
-        if noted:
-            relays.append((i, k, x_at))
+            target = jnp.where(place < z, lax.rem(z + 1, groups), lax.rem(z + groups - 1, groups))
+            hop(i, place, item, 1, target).start()
+
         if i < last:
-            send_x(i, place)
-        send_core(i, place, x_at)
-
-    def x_copy(i, place):
-        return remote(share_of(i, place, x), (x_send, x_recv), (i, place), x_peer)
-
-    def x_arrival(i, place):
-        return remote(share_of(i, place, 1 - x), (x_send, x_recv), (i, place), x_peer)
-
-    def core_copy(i, place, x_at):
-        return remote(share_of(i, place, x_at), (core_send, core_recv), (i, place, x_at), core_peer)
-
-    def send_x(i, place):
-        x_copy(i, place).start()
+            send_x(i, place, k)
+        send_core(i, place, 1 - x if item == layer_count else x)
+
+    def x_slot(i, k):
+        return [0, 1, 2 + i, 2 + last + i][k + 1] if i < last else 2 + 2 * last
+
+    def send_x(i, place, k):
+        remote(share_of(i, place, x), (x_send, i // last), (x_recv, x_slot(i, k)), x_peer).start()
 
     def send_core(i, place, x_at):
-        core_copy(i, place, x_at).start()
-
-    def cross(i, place):
-        x_arrival(i, place).wait_recv()
+        remote(share_of(i, place, x_at), (core_send, 0), (core_recv, i), core_peer).start()
+
+    def arrived_x(views, slot):
+        remote(twice(views), (x_send, 0), (x_recv, slot), x_peer).wait_recv()
+
+    def cross(i, k):
+        place = z if k < 0 else z_origins[k]
+        arrived_x(lambda: weights.at[i, place, 1 - x, core], x_slot(i, k))
         send_core(i, place, 1 - x)
+
+    def cross_wave(k):
+        place = z if k < 0 else z_origins[k]
+        arrived_x(lambda: weights.at[pl.ds(0, last), place, 1 - x, core], k + 1)
+        for i in range(last):
+            send_core(i, place, 1 - x)
 
     def send_share(i):
         @pl.when(solver)
         def _():
             shares[i].wait_recv()
 
-        spread(i, x)
-        send_x(i, z)
+        spread(i)
+        send_x(i, z, -1)
         send_core(i, z, x)
 
     share_order = [last] + list(range(last))
@@ -390,14 +406,14 @@
     @pl.when(solver)
     def _():
         for copy in edges:
-            start(copy, solver_sends)
+            copy.start()
         for load, c, copy in zip(out_loads, chunks, momenta):
             load.wait()
             got_out[:, c] = own_out[:, c].astype(narrow)
-            start(copy, solver_sends)
+            copy.start()
         hidden_load.wait()
         got_hidden[...] = own_hidden[...].astype(narrow)
-        start(hidden_momentum, solver_sends)
+        hidden_momentum.start()
 
     @pl.when(trainer)
     def _():
@@ -405,7 +421,7 @@
         for i in range(layer_count):
             weights[i, z, x, core] = own_hidden[i].astype(narrow)
         for i in share_order:
-            start(shares[i], trainer_sends)
+            shares[i].start()
 
     for i in share_order:
         send_share(i)
@@ -419,28 +435,29 @@
             copy.wait_recv()
         advance()
         for copy in fresh:
-            start(copy, solver_sends)
+            copy.start()
 
     @pl.when(trainer)
     def _():
-        for load, c in zip(out_loads, chunks):
-            load.wait()
-            out_ref[:, c] = own_out[:, c].astype(narrow)
-
-    pair_slots = [0]
-
-    def beside(views):
-        slot = pair_slots[0]
-        pair_slots[0] += 1
-        return remote(views, (pair_send, pair_recv), slot, core_peer)
-
-    tops = [beside(twice(lambda c=c: top.at[:, :, core, :, c])) for c in parts]
+        lent_target.start()
+        for j in reversed(range(count)):
+            out_loads[j].wait()
+            out_ref[:, chunks[j]] = own_out[:, chunks[j]].astype(narrow)
+            if j == lent:
+                lent_out.start()
+
+    def beside(views, kind, slot):
+        return remote(views, (pair_send, kind), (pair_recv, slot), core_peer)
+
+    tops = [beside(twice(lambda c=c: top.at[:, :, core, :, c]), 0, 0) for c in parts]
+    all_tops = beside(twice(lambda: top.at[:, :, core]), 0, 0)
     own_units = pl.ds(pl.multiple_of(core * unit_rows, unit_rows), unit_rows)
     other_units = pl.ds(pl.multiple_of((1 - core) * unit_rows, unit_rows), unit_rows)
     halves = [
-        beside(lambda i=i: (gradient.at[i, other_units, :], got_gradient.at[i]))
+        beside(lambda i=i: (gradient.at[i, other_units, :], got_gradient.at[i]), 1, 1 + i)
         for i in range(layer_count)
     ]
+    all_halves = beside(lambda: (gradient.at[:, other_units, :], got_gradient), 1, 1)
 
     def forward_columns(i, columns):
         block = weights[i, :, :, :, :, columns].reshape(width, COLUMNS)
@@ -453,68 +470,55 @@
         return result
 
     def forward(i):
+        for c in parts:
+            if i == last:
+                top[:, :, core, :, c] = forward_columns(i, c)
+            else:
+                inputs[i, :, :, :, c] = forward_columns(i, c)
         if i == last:
-            for c, copy in zip(parts, tops):
-                top[:, :, core, :, c] = forward_columns(i, c)
-                start(copy, sends)
-        else:
-
-            @pl.loop(0, width // COLUMNS)
-            def _(j):
-                columns = columns_of(j)
-                inputs[i, :, :, :, columns] = forward_columns(i, columns)
+            for copy in tops:
+                copy.start()
 
     def finish(i):
-        for place in range(groups):
-            for x_at in range(2):
-                arrival = remote(
-                    lambda place=place, x_at=x_at: (weights.at[i, place, x_at, 1 - core],) * 2,
-                    (core_send, core_recv),
-                    (i, place, x_at),
-                    core_peer,
-                )
-                arrival.wait_recv()
+        remote(
+            twice(lambda: weights.at[i, :, :, 1 - core]), (core_send, 0), (core_recv, i), core_peer
+        ).wait_recv()
         forward(i)
 
-    relay(last, 0, x)
-    cross(last, z)
-    spread(last, 1 - x)
+    relay(last, 0)
+    cross(last, -1)
+    spread(layer_count)
     for i in range(last):
-        relay(i, 0, x)
-    relay(last, 0, 1 - x)
-    for i in range(last):
-        cross(i, z)
-    items = [(i, x) for i in range(last)] + [(last, x), (last, 1 - x)]
-    for i, x_at in items:
-        relay(i, 1, x_at)
-    for i in range(last):
-        cross(i, z_origins[0])
-    inner = jnp.logical_and(z > 0, z < groups - 1)
+        relay(i, 0)
+    relay(layer_count, 0)
+    cross_wave(-1)
+    for item in range(layer_count + 1):
+        relay(item, 1)
+    cross_wave(0)
 
     @pl.when(inner)
     def _():
-        for i, x_at in items:
-            relay(i, 2, x_at)
-
-    for step, (i, x_at) in enumerate(items):
+        for item in range(layer_count + 1):
+            relay(item, 2)
+
+    for item in range(layer_count + 1):
 
         @pl.when(jnp.logical_not(inner))
         def _():
-            relay(i, 2, x_at, False)
-
-        if step < last:
-            cross(i, z_origins[1])
-        if step >= 2:
-            cross(step - 2, z_origins[2])
-            finish(step - 2)
+            relay(item, 2)
+
+        if item < last:
+            cross(item, 1)
+        if 1 <= item <= last:
+            cross(item - 1, 2)
+        if item >= 2:
+            finish(item - 2)
     finish(last)
 
     def update_out(j, decay, rate, other):
         c = chunks[j]
 
-        @pl.loop(0, width // COLUMNS)
-        def _(k):
-            units = columns_of(k)
+        for units in parts:
             grad = lax.dot_general(
                 top[:, :, :, :, units].reshape(batch, COLUMNS),
                 residual[:, :, :, :, c].reshape(batch, COLUMNS),
@@ -535,27 +539,42 @@
         momenta[j].wait_recv()
         update_out(j, momentum_decay, step_size, got_out)
 
-    x_sums, z_sums = [], []
-
-    def send_sum(views, j, slot, peer):
-        return start(remote(views, (sum_send, sum_recv), (j, slot), peer), trainer_sends)
+    def summed(views, kind, slot, peer):
+        return remote(views, (sum_send, kind), (sum_recv, slot), peer)
 
     core_sums = [
-        remote(
-            lambda c=c: (core_away.at[:, :, :, c], core_sum.at[:, :, :, c]),
-            (sum_send, sum_recv),
-            (j, 0),
-            core_peer,
-        )
+        summed(lambda c=c: (core_away.at[:, :, :, c], core_sum.at[:, :, :, c]), 0, j, core_peer)
         for j, c in enumerate(parts)
     ]
+    x_sums = [
+        summed(lambda c=c: (x_away.at[:, :, c], x_sum.at[:, :, c]), 1, len(parts) + j, x_peer)
+        for j, c in enumerate(pieces)
+    ]
+    z_base = len(parts) + len(pieces)
+    z_sums = [
+        [
+            summed(
+                lambda c=c, k=k: (z_away.at[z_places[k], :, c], z_sum.at[k, :, c]),
+                2,
+                z_base + j,
+                z_peers[k],
+            )
+            for k in range(groups - 1)
+        ]
+        for j, c in enumerate(pieces)
+    ]
+    others = pl.ds(0, groups - 1)
+    all_sums = [
+        summed(lambda: (core_away, core_sum), 0, 0, core_peer),
+        summed(lambda: (x_away, x_sum), 1, 0, x_peer),
+        summed(lambda: (z_away.at[others], z_sum), 2, 0, x_peer),
+    ]
     targets = own_fields.reshape(groups, 2, 2, rows, cells)
 
-    def residual_columns(side, c):
+    def residual_columns(side, c, wanted):
         rows_of = top[:, :, side].reshape(half, width)
         predicted = jnp.dot(rows_of, out_ref[:, c], preferred_element_type=wide)
-        wanted = targets[:, :, side, :, c].reshape(half, COLUMNS)
-        kept = ((predicted - wanted) / batch).astype(narrow)
+        kept = ((predicted - wanted.reshape(half, COLUMNS)) / batch).astype(narrow)
         residual[:, :, side, :, c] = kept.reshape(groups, 2, rows, COLUMNS)
 
     def upstream_columns(side, c):
@@ -569,26 +588,22 @@
     @pl.when(trainer)
     def _():
         for c in chunks:
-            residual_columns(core, c)
-        for copy in tops:
-            copy.wait_recv()
-        for j, c in enumerate(chunks):
-            residual_columns(1 - core, c)
-            if j < 2:
-                start(residuals[j], trainer_sends)
-        for c, copy in zip(parts, core_sums):
+            residual_columns(core, c, targets[:, :, core, :, c])
+        all_tops.wait_recv()
+        for c in chunks:
+            residual_columns(1 - core, c, targets[:, :, 1 - core, :, c])
+        for copy in residuals:
+            copy.start()
+        for c in parts:
             core_away[:, :, :, c] = upstream_columns(1 - core, c)
-            start(copy, trainer_sends)
+        for copy in core_sums:
+            copy.start()
         for j, c in enumerate(parts):
             partial[:, :, :, c] = upstream_columns(core, c)
             core_sums[j].wait_recv()
             x_away[:, :, c] = (partial[:, 1 - x, :, c] + core_sum[:, 1 - x, :, c]).astype(narrow)
-            for q in range(j * per_part, (j + 1) * per_part):
-                x_sums.append(
-                    send_sum(
-                        lambda c=pieces[q]: (x_away.at[:, :, c], x_sum.at[:, :, c]), q, 1, x_peer
-                    )
-                )
+            for copy in x_sums[j * per_part : (j + 1) * per_part]:
+                copy.start()
         update_trainer(0)
         for j, c in enumerate(pieces):
             near = partial[:, x, :, c] + core_sum[:, x, :, c]
@@ -596,66 +611,69 @@
             near = near + x_sum[:, :, c].astype(wide)
             partial[:, x, :, c] = near
             z_away[:, :, c] = near.astype(narrow)
-            z_sums.append(
-                [
-                    send_sum(
-                        lambda c=c, k=k: (z_away.at[z_places[k], :, c], z_sum.at[k, :, c]),
-                        j,
-                        2 + k,
-                        z_peers[k],
-                    )
-                    for k in range(groups - 1)
-                ]
-            )
+            for copy in z_sums[j]:
+                copy.start()
         update_trainer(1)
 
     @pl.when(solver)
     def _():
-        for copy in tops:
-            copy.wait_recv()
-        update_solver(0)
-        update_solver(1)
-
-    def send_slope(view, j, slot, peer):
-        return start(remote(twice(view), (slope_send, slope_recv), (j, slot), peer), sends)
-
-    z_slopes, x_slopes = [], []
+        all_tops.wait_recv()
+        lent_out.wait_recv()
+        lent_target.wait_recv()
+        lent_wanted = lent_fields.reshape(groups, 2, 2, rows, cells - lent * COLUMNS)
+        for j in range(lent, count):
+            for side in range(2):
+                residual_columns(side, chunks[j], lent_wanted[:, :, side, :, chunks[j - lent]])
+        for j in range(lent, count):
+            update_out(j, momentum_decay, None, None)
+        for j in range(lent):
+            update_solver(j)
+
+    def z_slope(c, slot, peer):
+        return remote(
+            twice(lambda: slope.at[z, x, :, c]), (slope_send, 0), (slope_recv, slot), peer
+        )
+
     for j, c in enumerate(pieces):
 
         @pl.when(trainer)
         def _():
+            summed(
+                lambda: (z_away.at[others, :, c], z_sum.at[:, :, c]), 2, z_base + j, x_peer
+            ).wait_recv()
             upstream = partial[z, x, :, c]
             for k in range(groups - 1):
-                z_sums[j][k].wait_recv()
                 upstream = upstream + z_sum[k, :, c].astype(wide)
             slope[z, x, :, c] = (upstream * factors[last, z, x, :, c]).astype(narrow)
-            start(slope_shares[j], trainer_sends)
+            slope_shares[j].start()
 
         @pl.when(solver)
         def _():
             slope_shares[j].wait_recv()
 
-        view = lambda c=c: slope.at[z, x, :, c]
-        z_slopes.append([send_slope(view, j, k, z_peers[k]) for k in range(groups - 1)])
+        for peer in z_peers:
+            z_slope(c, j, peer).start()
 
     @pl.when(trainer)
     def _():
-        for copy in residuals[2:]:
-            start(copy, trainer_sends)
         update_trainer(2)
 
+    def x_slope(view):
+        return remote(twice(view), (slope_send, 1), (slope_recv, len(pieces)), x_peer)
+
     for j, c in enumerate(pieces):
-        for copy in z_slopes[j]:
-            copy.wait_recv()
-        x_slopes.append(send_slope(lambda c=c: slope.at[:, x, :, c], j, groups - 1, x_peer))
+        remote(
+            twice(lambda: slope.at[others, x, :, c]), (slope_send, 0), (slope_recv, j), x_peer
+        ).wait_recv()
+        x_slope(lambda: slope.at[:, x, :, c]).start()
 
     @pl.when(trainer)
     def _():
         update_trainer(3)
         hidden_momentum.wait_recv()
 
-    for copy in x_slopes:
-        copy.wait_recv()
+    all_x_slopes = x_slope(lambda: slope.at[:, 1 - x])
+    all_x_slopes.wait_recv()
 
     first_lane = pl.multiple_of((tile // 2) * LANES, LANES)
 
@@ -676,47 +694,33 @@
     for step, i in enumerate(reversed(range(layer_count))):
         this_slope = slopes[0] if step == 0 else slopes[1 + step % 2]
         next_slope = slopes[1 + (step + 1) % 2]
-        if i > 0:
-
-            @pl.loop(0, width // COLUMNS)
-            def _(j):
-                columns = columns_of(j)
-                block = weights.at[i].reshape(width, width)[columns, :]
+        lanes = pl.ds(first_lane, LANES)
+        own_inputs = features_ref[:, :, core, :, lanes] if i == 0 else inputs[i - 1, :, :, :, lanes]
+        for c in parts:
+            if i > 0:
                 back = lax.dot_general(
                     this_slope[...].reshape(half, width),
-                    block,
+                    weights.at[i].reshape(width, width)[c, :],
                     (((1,), (1,)), ((), ())),
                     preferred_element_type=wide,
                 )
-                factor = factors[i - 1, :, :, :, columns].reshape(half, COLUMNS)
-                next_slope[:, :, :, columns] = (
+                factor = factors[i - 1, :, :, :, c].reshape(half, COLUMNS)
+                next_slope[:, :, :, c] = (
                     (back * factor).astype(narrow).reshape(groups, 2, rows, COLUMNS)
                 )
-
-        lanes = pl.ds(first_lane, LANES)
-        own_inputs = features_ref[:, :, core, :, lanes] if i == 0 else inputs[i - 1, :, :, :, lanes]
-
-        @pl.loop(0, width // COLUMNS)
-        def _(j):
-            columns = columns_of(j)
-            gradient[i, :, columns] = lax.dot_general(
+            gradient[i, :, c] = lax.dot_general(
                 own_inputs.reshape(half, LANES),
-                this_slope[:, :, :, columns].reshape(half, COLUMNS),
+                this_slope[:, :, :, c].reshape(half, COLUMNS),
                 (((0,), (0,)), ((), ())),
                 preferred_element_type=wide,
             )
-
-        start(halves[i], sends)
+        halves[i].start()
         if i < last:
             update_hidden(i + 1)
 
-    @pl.when(solver)
-    def _():
-        for j in range(2, len(chunks)):
-            update_solver(j)
-
     @pl.when(trainer)
     def _():
+        lent_target.wait_send()
         member = lax.broadcasted_iota(jnp.int32, (batch, batch), 0)
         chosen = jnp.where(member == assignment_ref[...], 1.0, 0.0).astype(narrow)
         for j, c in enumerate(chunks):
@@ -727,40 +731,41 @@
 
     update_hidden(0)
 
-    for copy in sends:
-        copy.wait_send()
-    for i in range(layer_count):
-        for place in range(groups):
-            if i < last:
-                x_copy(i, place).wait_send()
-            for x_at in range(2):
-                core_copy(i, place, x_at).wait_send()
-    x_copy(last, z).wait_send()
-    for i, x_at in spreads:
-
-        @pl.when(z < groups - 1)
-        def _():
-            hop(i, z, x_at, 0, above).wait_send()
-
-        @pl.when(z > 0)
-        def _():
-            hop(i, z, x_at, 1, below).wait_send()
-
-    for i, k, x_at in relays:
-
-        @pl.when(onward(k))
-        def _():
-            hop(i, z_origins[k], x_at, 0, above).wait_send()
+    def gone(view, semaphore, slot):
+        remote(twice(view), (semaphore, slot), (x_recv, 0), x_peer).wait_send()
+
+    gone(lambda: weights.at[:, :, :, core], core_send, 0)
+    gone(lambda: weights.at[pl.ds(0, last), :, x, core], x_send, 0)
+    gone(lambda: weights.at[last, z, x, core], x_send, 1)
+    gone(lambda: weights.at[:, z, x, core], z_send, 0)
+    gone(lambda: weights.at[last, z, x, core], z_send, 2)
+
+    @pl.when(inner)
+    def _():
+        gone(lambda: weights.at[:, :, x, core], z_send, 1)
+        gone(lambda: weights.at[last, :, x, core], z_send, 3)
+
+    all_tops.wait_send()
+    all_halves.wait_send()
+    gone(lambda: slope.at[others, x], slope_send, 0)
+    gone(lambda: slope.at[:, x], slope_send, 1)
 
     @pl.when(solver)
     def _():
-        for copy in solver_sends:
+        for copy in edges:
             copy.wait_send()
+        gone(lambda: got_out, role_send, 0)
+        gone(lambda: got_hidden, role_send, 1)
+        gone(lambda: got_fields, role_send, 2)
 
     @pl.when(trainer)
     def _():
-        for copy in trainer_sends:
+        for copy in all_sums:
             copy.wait_send()
+        gone(lambda: weights.at[:, z, x, core], role_send, 0)
+        gone(lambda: out_ref.at[:, lent_cells], role_send, 1)
+        gone(lambda: residual.at[:, :, :, :, pl.ds(0, lent * COLUMNS)], role_send, 3)
+        gone(lambda: slope.at[z, x], role_send, 4)
 
 
 def fused_step(fields, velocity, growth, features, assignment, own_out, own_hidden):
@@ -772,6 +777,7 @@
     dma = pltpu.SemaphoreType.DMA
     anywhere = pl.BlockSpec(memory_space=pltpu.HBM)
     parts, pieces = width // COLUMNS, cells // COLUMNS
+    splits = width // LANES
     splits = width // LANES
     role_slots = layer_count + 3 * pieces + 1 + splits
     split = (groups, 2, 2, rows, width)
@@ -792,6 +798,7 @@
             pltpu.VMEM((1, LANES), wide),
             pltpu.VMEM((batch, LANES), wide),
             pltpu.VMEM((batch, LANES), wide),
+            pltpu.VMEM((batch, cells // 2), wide),
             pltpu.VMEM((width, cells), narrow),
             pltpu.VMEM((width, cells), narrow),
             pltpu.VMEM(own_hidden.shape, narrow),
@@ -813,20 +820,20 @@
             pltpu.VMEM((groups, rows, width), narrow),
             pltpu.VMEM((groups, rows, width), narrow),
             pltpu.VMEM((groups - 1, rows, width), narrow),
-            dma((layer_count, groups, 2, 2)),
-            dma((layer_count, groups, 2)),
-            dma((layer_count, groups)),
-            dma((layer_count, groups)),
-            dma((layer_count, groups, 2)),
-            dma((layer_count, groups, 2)),
-            dma((splits, groups + 1)),
-            dma((splits, groups + 1)),
-            dma((splits, groups)),
-            dma((splits, groups)),
-            dma((role_slots,)),
-            dma((role_slots,)),
-            dma((parts + layer_count,)),
-            dma((parts + layer_count,)),
+            dma((4,)),
+            dma((layer_count + 1, groups - 1)),
+            dma((2,)),
+            dma((2 * layer_count + 1,)),
+            dma((1,)),
+            dma((layer_count,)),
+            dma((3,)),
+            dma((parts + 2 * splits,)),
+            dma((2,)),
+            dma((splits + 1,)),
+            dma((5,)),
+            dma((layer_count + 2 + pieces // 2 + splits,)),
+            dma((2,)),
+            dma((1 + layer_count,)),
             dma((3,)),
             dma((3,)),
             dma((6 + pieces,)),

time: 112 us -> 101 us (0.902)
  Pallas kernels: 107 us -> 96.1 us
    pallas_call x1, Pallas kernels: 107 us -> 96.1 us  [fused_step(): pl.pallas_call(functools.partial(train_kernel, groups), out_shape=(jax.Sh...]
where the time goes in v4:
time: 101 us
  Pallas kernels  96.1 us (95%)
  local copies, waits for them, and re-layouts  4.39 us (4%)
    pallas_call x1, Pallas kernels, fused_step(): pl.pallas_call(functools.partial(train_kernel, groups), out_shape=(jax.Sh...  96.1 us
    unnamed x3, local copies, waits for them, and re-layouts  4.39 us

profile of v4, /device:TPU:0, one launch (start us, length us, event | category | flops | bytes accessed | tf_op | source)
XLA Modules:
  0.0 101.1 jit_solution(15226568974251970194)
XLA Ops:
  0.6 96.1 %shard_map.94 = (f32[512,1024]{1,0:T(8,128)S(1)}, f32[1024,1024]{1,0:T(8,128)S(1)}, f32[5,64,1024]{2,1,0:T(8,128)S(1)}) custom-call(bf16[4,2,2,32,1024]{4,3,2,1,0:T(8,128)(2,1)} %bitcast.16, f32[512,1024]{1,0:T(8,128)} %bitcast.14, f32[1,1024]{1,0:T(1,128)} %bitcast.17, f32[1,1024]{1,0:T(1,128)} %bitcast.18, s32[1,512]{1,0:T(1,128)} %bitcast.19, ...), custom_call_target="tpu_custom_call" | custom-call | flops 32212254720 | bytes 20971520 | tf_op jit(solution)/shard_map/pallas_call | solution.py:784
  96.8 1.3 %copy.13 = f32[1,512,1024]{2,1,0:T(8,128)} copy(f32[1,512,1024]{2,1,0:T(8,128)S(1)} %bitcast.11) | data formatting | bytes 4194304
  98.1 2.0 %copy.14 = f32[1,1024,1024]{2,1,0:T(8,128)} copy(f32[1,1024,1024]{2,1,0:T(8,128)S(1)} %bitcast.10) | data formatting | bytes 8388608
  100.1 1.1 %copy.15 = f32[1,5,64,1024]{3,2,1,0:T(8,128)} copy(f32[1,5,64,1024]{3,2,1,0:T(8,128)S(1)} %bitcast.12) | data formatting | bytes 2621440

commit v5 on v4

--- a/solution.py
+++ b/solution.py
@@ -89,6 +89,9 @@
 
 LANES = 128
 COLUMNS = 256
+
+
+LAG = 3
 
 
 class Later:
@@ -367,7 +370,8 @@
         def _():
             shares[i].wait_recv()
 
-        spread(i)
+        if i < last:
+            spread(i)
         send_x(i, z, -1)
         send_core(i, z, x)
 
@@ -485,34 +489,74 @@
         ).wait_recv()
         forward(i)
 
-    relay(last, 0)
+    outer = jnp.logical_not(inner)
+    lagging = [last, layer_count]
+
+    @pl.when(inner)
+    def _():
+        for item in range(last):
+            relay(item, 0)
+            relay(item, 1)
+
+    @pl.when(outer)
+    def _():
+        for item in range(last):
+            relay(item, 0)
+
+    spread(last)
     cross(last, -1)
+    cross_wave(-1)
+
+    @pl.when(inner)
+    def _():
+        for item in range(last):
+            relay(item, 2)
+
+    @pl.when(outer)
+    def _():
+        for item in range(last):
+            relay(item, 1)
+
     spread(layer_count)
-    for i in range(last):
-        relay(i, 0)
-    relay(layer_count, 0)
-    cross_wave(-1)
-    for item in range(layer_count + 1):
-        relay(item, 1)
     cross_wave(0)
 
     @pl.when(inner)
     def _():
-        for item in range(layer_count + 1):
-            relay(item, 2)
-
-    for item in range(layer_count + 1):
-
-        @pl.when(jnp.logical_not(inner))
+        for k in range(2):
+            for item in lagging:
+                relay(item, k)
+
+    for item in range(last):
+
+        @pl.when(outer)
         def _():
             relay(item, 2)
 
-        if item < last:
-            cross(item, 1)
-        if 1 <= item <= last:
-            cross(item - 1, 2)
-        if item >= 2:
-            finish(item - 2)
+        cross(item, 1)
+
+    @pl.when(inner)
+    def _():
+        for item in lagging:
+            relay(item, 2)
+
+    held = [(item, k) for k in range(groups - 1) for item in lagging]
+    for i in range(last):
+
+        @pl.when(outer)
+        def _():
+            for item, k in [held[:2], held[2:3], held[3:4], held[4:5]][i]:
+                relay(item, k)
+
+        cross(i, 2)
+        if i > 0:
+            finish(i - 1)
+    finish(last - 1)
+
+    @pl.when(outer)
+    def _():
+        for item, k in held[5:]:
+            relay(item, k)
+
     finish(last)
 
     def update_out(j, decay, rate, other):
@@ -589,31 +633,25 @@
     def _():
         for c in chunks:
             residual_columns(core, c, targets[:, :, core, :, c])
+        early = len(parts) // 2
+        for c in parts[:early]:
+            partial[:, :, :, c] = upstream_columns(core, c)
         all_tops.wait_recv()
         for c in chunks:
             residual_columns(1 - core, c, targets[:, :, 1 - core, :, c])
-        for copy in residuals:
-            copy.start()
+        residuals[0].start()
         for c in parts:
             core_away[:, :, :, c] = upstream_columns(1 - core, c)
         for copy in core_sums:
             copy.start()
+        for c in parts[early:]:
+            partial[:, :, :, c] = upstream_columns(core, c)
         for j, c in enumerate(parts):
-            partial[:, :, :, c] = upstream_columns(core, c)
             core_sums[j].wait_recv()
             x_away[:, :, c] = (partial[:, 1 - x, :, c] + core_sum[:, 1 - x, :, c]).astype(narrow)
             for copy in x_sums[j * per_part : (j + 1) * per_part]:
                 copy.start()
         update_trainer(0)
-        for j, c in enumerate(pieces):
-            near = partial[:, x, :, c] + core_sum[:, x, :, c]
-            x_sums[j].wait_recv()
-            near = near + x_sum[:, :, c].astype(wide)
-            partial[:, x, :, c] = near
-            z_away[:, :, c] = near.astype(narrow)
-            for copy in z_sums[j]:
-                copy.start()
-        update_trainer(1)
 
     @pl.when(solver)
     def _():
@@ -626,46 +664,70 @@
                 residual_columns(side, chunks[j], lent_wanted[:, :, side, :, chunks[j - lent]])
         for j in range(lent, count):
             update_out(j, momentum_decay, None, None)
-        for j in range(lent):
-            update_solver(j)
 
     def z_slope(c, slot, peer):
         return remote(
             twice(lambda: slope.at[z, x, :, c]), (slope_send, 0), (slope_recv, slot), peer
         )
 
-    for j, c in enumerate(pieces):
-
-        @pl.when(trainer)
-        def _():
-            summed(
-                lambda: (z_away.at[others, :, c], z_sum.at[:, :, c]), 2, z_base + j, x_peer
-            ).wait_recv()
-            upstream = partial[z, x, :, c]
-            for k in range(groups - 1):
-                upstream = upstream + z_sum[k, :, c].astype(wide)
-            slope[z, x, :, c] = (upstream * factors[last, z, x, :, c]).astype(narrow)
-            slope_shares[j].start()
-
-        @pl.when(solver)
-        def _():
-            slope_shares[j].wait_recv()
-
-        for peer in z_peers:
-            z_slope(c, j, peer).start()
-
-    @pl.when(trainer)
-    def _():
-        update_trainer(2)
-
     def x_slope(view):
         return remote(twice(view), (slope_send, 1), (slope_recv, len(pieces)), x_peer)
 
-    for j, c in enumerate(pieces):
+    def add_far(j, c):
+        near = partial[:, x, :, c] + core_sum[:, x, :, c]
+        x_sums[j].wait_recv()
+        near = near + x_sum[:, :, c].astype(wide)
+        partial[:, x, :, c] = near
+        z_away[:, :, c] = near.astype(narrow)
+        for copy in z_sums[j]:
+            copy.start()
+
+    def make_slope(j, c):
+        summed(
+            lambda: (z_away.at[others, :, c], z_sum.at[:, :, c]), 2, z_base + j, x_peer
+        ).wait_recv()
+        upstream = partial[z, x, :, c]
+        for k in range(groups - 1):
+            upstream = upstream + z_sum[k, :, c].astype(wide)
+        slope[z, x, :, c] = (upstream * factors[last, z, x, :, c]).astype(narrow)
+        slope_shares[j].start()
+
+    def pass_slope(j, c):
         remote(
             twice(lambda: slope.at[others, x, :, c]), (slope_send, 0), (slope_recv, j), x_peer
         ).wait_recv()
         x_slope(lambda: slope.at[:, x, :, c]).start()
+
+    for turn in range(len(pieces) + 2 * LAG):
+        made, passed = turn - LAG, turn - 2 * LAG
+
+        @pl.when(trainer)
+        def _():
+            if turn < len(pieces):
+                add_far(turn, pieces[turn])
+            if turn == len(pieces) // 2:
+                update_trainer(1)
+            if 0 <= made < len(pieces):
+                make_slope(made, pieces[made])
+            if made == len(pieces) - 1:
+                for copy in residuals[1:]:
+                    copy.start()
+                update_trainer(2)
+
+        if 0 <= made < len(pieces):
+
+            @pl.when(solver)
+            def _():
+                slope_shares[made].wait_recv()
+
+            for peer in z_peers:
+                z_slope(pieces[made], made, peer).start()
+        if passed >= 0:
+            pass_slope(passed, pieces[passed])
+
+    @pl.when(solver)
+    def _():
+        update_solver(0)
 
     @pl.when(trainer)
     def _():
@@ -715,8 +777,13 @@
                 preferred_element_type=wide,
             )
         halves[i].start()
-        if i < last:
-            update_hidden(i + 1)
+        if i < last - 1:
+            update_hidden(i + 2)
+
+    @pl.when(solver)
+    def _():
+        for j in range(1, lent):
+            update_solver(j)
 
     @pl.when(trainer)
     def _():
@@ -729,6 +796,7 @@
                 chosen, got_fields[:, c], (((0,), (0,)), ((), ())), preferred_element_type=wide
             )
 
+    update_hidden(1)
     update_hidden(0)
 
     def gone(view, semaphore, slot):
@@ -766,6 +834,18 @@
         gone(lambda: out_ref.at[:, lent_cells], role_send, 1)
         gone(lambda: residual.at[:, :, :, :, pl.ds(0, lent * COLUMNS)], role_send, 3)
         gone(lambda: slope.at[z, x], role_send, 4)
+
+
+def store_kernel(*refs):
+    semaphores = refs[-1]
+    copies = [
+        pltpu.make_async_copy(source, target, semaphores.at[k])
+        for k, (source, target) in enumerate(zip(refs[:3], refs[3:6]))
+    ]
+    for copy in copies:
+        copy.start()
+    for copy in copies:
+        copy.wait()
 
 
 def fused_step(fields, velocity, growth, features, assignment, own_out, own_hidden):
@@ -775,13 +855,13 @@
     rows = batch // lax.axis_size("tile")
     narrow, wide = jnp.bfloat16, jnp.float32
     dma = pltpu.SemaphoreType.DMA
-    anywhere = pl.BlockSpec(memory_space=pltpu.HBM)
+    anywhere = pl.BlockSpec(memory_space=pl.ANY)
     parts, pieces = width // COLUMNS, cells // COLUMNS
     splits = width // LANES
     splits = width // LANES
     role_slots = layer_count + 3 * pieces + 1 + splits
     split = (groups, 2, 2, rows, width)
-    return pl.pallas_call(
+    results = pl.pallas_call(
         functools.partial(train_kernel, groups),
         out_shape=(
             jax.ShapeDtypeStruct(fields.shape, wide),
@@ -858,6 +938,14 @@
             )
         )
     )
+    return pl.pallas_call(
+        store_kernel,
+        out_shape=tuple(jax.ShapeDtypeStruct(v.shape, v.dtype) for v in results),
+        in_specs=[anywhere] * 3,
+        out_specs=[anywhere] * 3,
+        scratch_shapes=[dma((3,))],
+        compiler_params=pltpu.CompilerParams(vmem_limit_bytes=1 << 20),
+    )(*results)
 
 
 def plain_body(fields_pair, velocity, growth, features, assignment, out_pair, hidden_pair):
@@ -901,7 +989,7 @@
     fits = (
         lax.axis_size("role") == 2
         and tiles == 16
-        and layer_count > 2
+        and layer_count == 5
         and batch % tiles == 0
         and (batch // tiles) % 16 == 0
         and LANES == 2 * unit_rows

time: 101 us -> 98.1 us (0.971)
  local copies, waits for them, and re-layouts: 4.39 us -> 0 us
  Pallas kernels: 96.1 us -> 97.2 us
    unnamed x3 -> x0, local copies, waits for them, and re-layouts: 4.39 us -> none
    pallas_call x0 -> x1, Pallas kernels: none -> 3.15 us  [fused_step(): pl.pallas_call(store_kernel, out_shape=tuple((jax.ShapeDtypeStruct(v.shap...]
    pallas_call x1, Pallas kernels: 96.1 us -> 94 us  [fused_step(): pl.pallas_call(functools.partial(train_kernel, groups), out_shape=(jax.Sh...]
where the time goes in v5:
time: 98.1 us; the launch traced here: 98 us
  Pallas kernels  97.2 us (99%)
    pallas_call x1, Pallas kernels, fused_step(): pl.pallas_call(functools.partial(train_kernel, groups), out_shape=(jax.Sh...  94 us
    pallas_call x1, Pallas kernels, fused_step(): pl.pallas_call(store_kernel, out_shape=tuple((jax.ShapeDtypeStruct(v.shap...  3.15 us

profile of v5, /device:TPU:0, one launch (start us, length us, event | category | flops | bytes accessed | tf_op | source)
XLA Modules:
  0.0 98.0 jit_solution(15026093165334638124)
XLA Ops:
  0.6 94.0 %shard_map.94 = (f32[512,1024]{1,0:T(8,128)S(1)}, f32[1024,1024]{1,0:T(8,128)S(1)}, f32[5,64,1024]{2,1,0:T(8,128)S(1)}) custom-call(bf16[4,2,2,32,1024]{4,3,2,1,0:T(8,128)(2,1)} %bitcast.16, f32[512,1024]{1,0:T(8,128)} %bitcast.12, f32[1,1024]{1,0:T(1,128)} %bitcast.17, f32[1,1024]{1,0:T(1,128)} %bitcast.18, s32[1,512]{1,0:T(1,128)} %bitcast.19, ...), custom_call_target="tpu_custom_call" | custom-call | flops 32212254720 | bytes 20971520 | tf_op jit(solution)/shard_map/pallas_call | solution.py:864
  94.6 3.2 %shard_map.95 = (f32[512,1024]{1,0:T(8,128)}, f32[1024,1024]{1,0:T(8,128)}, f32[5,64,1024]{2,1,0:T(8,128)}) custom-call(f32[512,1024]{1,0:T(8,128)S(1)} %get-tuple-element.9.refs_0_, f32[1024,1024]{1,0:T(8,128)S(1)} %get-tuple-element.10.refs_1_, f32[5,64,1024]{2,1,0:T(8,128)S(1)} %get-tuple-element.11.refs_2_), custom_call_target="tpu_custom_call" | custom-call | tf_op jit(solution)/shard_map/pallas_call | solution.py:941

commit v6 on v5

--- a/solution.py
+++ b/solution.py
@@ -91,7 +91,8 @@
 COLUMNS = 256
 
 
-LAG = 3
+SUM_LAG = 7
+PASS_LAG = 7
 
 
 class Later:
@@ -131,6 +132,7 @@
     left_edge,
     right_edge,
     lent_fields,
+    chosen_ref,
     out_ref,
     got_out,
     got_hidden,
@@ -266,10 +268,23 @@
     for load in loads:
         load.start()
     hidden_load, out_loads, small_loads = loads[0], loads[1 : 1 + len(chunks)], loads[1 + len(chunks) :]
+    share_order = [last] + list(range(last))
     barrier = pltpu.get_barrier_semaphore()
     peers = z_peers + [x_peer, core_peer, role_peer, far_peer]
     for peer in peers:
         pl.semaphore_signal(barrier, inc=1, device_id=peer, device_id_type=pl.DeviceIdType.MESH)
+
+    @pl.when(solver)
+    def _():
+        out_loads[0].wait()
+        got_out[:, chunks[0]] = own_out[:, chunks[0]].astype(narrow)
+
+    @pl.when(trainer)
+    def _():
+        hidden_load.wait()
+        for i in share_order:
+            weights[i, z, x, core] = own_hidden[i].astype(narrow)
+
     pl.semaphore_wait(barrier, len(peers))
 
     last_lanes = pl.ds(cells - LANES, LANES)
@@ -375,7 +390,6 @@
         send_x(i, z, -1)
         send_core(i, z, x)
 
-    share_order = [last] + list(range(last))
 
     def columns_of(j):
         return pl.ds(pl.multiple_of(j * COLUMNS, COLUMNS), COLUMNS)
@@ -409,21 +423,21 @@
 
     @pl.when(solver)
     def _():
+        momenta[0].start()
         for copy in edges:
             copy.start()
-        for load, c, copy in zip(out_loads, chunks, momenta):
-            load.wait()
-            got_out[:, c] = own_out[:, c].astype(narrow)
-            copy.start()
-        hidden_load.wait()
-        got_hidden[...] = own_hidden[...].astype(narrow)
-        hidden_momentum.start()
+        for j in range(1, count):
+            out_loads[j].wait()
+            got_out[:, chunks[j]] = own_out[:, chunks[j]].astype(narrow)
+            if j < lent:
+                momenta[j].start()
+            if j == lent - 1:
+                hidden_load.wait()
+                got_hidden[...] = own_hidden[...].astype(narrow)
+                hidden_momentum.start()
 
     @pl.when(trainer)
     def _():
-        hidden_load.wait()
-        for i in range(layer_count):
-            weights[i, z, x, core] = own_hidden[i].astype(narrow)
         for i in share_order:
             shares[i].start()
 
@@ -438,7 +452,7 @@
         for copy in edges:
             copy.wait_recv()
         advance()
-        for copy in fresh:
+        for copy in fresh + momenta[lent:]:
             copy.start()
 
     @pl.when(trainer)
@@ -449,6 +463,9 @@
             out_ref[:, chunks[j]] = own_out[:, chunks[j]].astype(narrow)
             if j == lent:
                 lent_out.start()
+        member = lax.broadcasted_iota(jnp.int32, (batch, batch), 0)
+        chosen = jnp.where(member == assignment_ref[...], 1.0, 0.0)
+        chosen_ref[...] = chosen.T.astype(narrow)
 
     def beside(views, kind, slot):
         return remote(views, (pair_send, kind), (pair_recv, slot), core_peer)
@@ -474,14 +491,14 @@
         return result
 
     def forward(i):
-        for c in parts:
-            if i == last:
-                top[:, :, core, :, c] = forward_columns(i, c)
-            else:
+        for j, c in enumerate(parts):
+            if i < last:
                 inputs[i, :, :, :, c] = forward_columns(i, c)
-        if i == last:
-            for copy in tops:
-                copy.start()
+                continue
+            top[:, :, core, :, c] = forward_columns(i, c)
+            if j % 2:
+                tops[j - 1].start()
+                tops[j].start()
 
     def finish(i):
         remote(
@@ -569,8 +586,10 @@
                 (((0,), (0,)), ((), ())),
                 preferred_element_type=wide,
             )
-            if other is None:
+            if rate is None:
                 own_out[units, c] = decay * own_out[units, c] + grad
+            elif other is None:
+                own_out[units, c] = own_out[units, c] - rate * grad
             else:
                 fresh_momentum = decay * other[units, c].astype(wide) + grad
                 own_out[units, c] = own_out[units, c] - rate * fresh_momentum
@@ -580,8 +599,21 @@
         update_out(j, momentum_decay, None, None)
 
     def update_trainer(j):
+        if j < lent:
+            momenta[j].wait_recv()
+        update_out(j, momentum_decay, step_size, got_out if j < lent else None)
+
+    def add_momentum(j):
         momenta[j].wait_recv()
-        update_out(j, momentum_decay, step_size, got_out)
+        for units in parts:
+            late = momentum_decay * got_out[units, chunks[j]].astype(wide)
+            own_out[units, chunks[j]] = own_out[units, chunks[j]] - step_size * late
+
+    def gather(j):
+        fresh[j].wait_recv()
+        own_fields[:, chunks[j]] = jnp.dot(
+            chosen_ref[...], got_fields[:, chunks[j]], preferred_element_type=wide
+        )
 
     def summed(views, kind, slot, peer):
         return remote(views, (sum_send, kind), (sum_recv, slot), peer)
@@ -652,6 +684,9 @@
             for copy in x_sums[j * per_part : (j + 1) * per_part]:
                 copy.start()
         update_trainer(0)
+        lent_target.wait_send()
+        for j in range(lent):
+            gather(j)
 
     @pl.when(solver)
     def _():
@@ -664,6 +699,7 @@
                 residual_columns(side, chunks[j], lent_wanted[:, :, side, :, chunks[j - lent]])
         for j in range(lent, count):
             update_out(j, momentum_decay, None, None)
+        update_solver(0)
 
     def z_slope(c, slot, peer):
         return remote(
@@ -698,8 +734,8 @@
         ).wait_recv()
         x_slope(lambda: slope.at[:, x, :, c]).start()
 
-    for turn in range(len(pieces) + 2 * LAG):
-        made, passed = turn - LAG, turn - 2 * LAG
+    for turn in range(len(pieces) + SUM_LAG + PASS_LAG):
+        made, passed = turn - SUM_LAG, turn - SUM_LAG - PASS_LAG
 
         @pl.when(trainer)
         def _():
@@ -712,7 +748,8 @@
             if made == len(pieces) - 1:
                 for copy in residuals[1:]:
                     copy.start()
-                update_trainer(2)
+                for j in range(lent, count):
+                    gather(j)
 
         if 0 <= made < len(pieces):
 
@@ -725,14 +762,16 @@
         if passed >= 0:
             pass_slope(passed, pieces[passed])
 
+    @pl.when(trainer)
+    def _():
+        for j in range(lent, count):
+            update_trainer(j)
+        hidden_momentum.wait_recv()
+
     @pl.when(solver)
     def _():
-        update_solver(0)
-
-    @pl.when(trainer)
-    def _():
-        update_trainer(3)
-        hidden_momentum.wait_recv()
+        for j in range(1, lent):
+            update_solver(j)
 
     all_x_slopes = x_slope(lambda: slope.at[:, 1 - x])
     all_x_slopes.wait_recv()
@@ -780,21 +819,10 @@
         if i < last - 1:
             update_hidden(i + 2)
 
-    @pl.when(solver)
-    def _():
-        for j in range(1, lent):
-            update_solver(j)
-
     @pl.when(trainer)
     def _():
-        lent_target.wait_send()
-        member = lax.broadcasted_iota(jnp.int32, (batch, batch), 0)
-        chosen = jnp.where(member == assignment_ref[...], 1.0, 0.0).astype(narrow)
-        for j, c in enumerate(chunks):
-            fresh[j].wait_recv()
-            own_fields[:, c] = lax.dot_general(
-                chosen, got_fields[:, c], (((0,), (0,)), ((), ())), preferred_element_type=wide
-            )
+        for j in range(lent, count):
+            add_momentum(j)
 
     update_hidden(1)
     update_hidden(0)
@@ -838,10 +866,17 @@
 
 def store_kernel(*refs):
     semaphores = refs[-1]
-    copies = [
-        pltpu.make_async_copy(source, target, semaphores.at[k])
-        for k, (source, target) in enumerate(zip(refs[:3], refs[3:6]))
-    ]
+    copies = []
+    for source, target in zip(refs[:3], refs[3:6]):
+        length = source.shape[0]
+        step = length if length % 4 else length // 4
+        for at in range(0, length, step):
+            band = pl.ds(at, step)
+            copies.append(
+                pltpu.make_async_copy(
+                    source.at[band], target.at[band], semaphores.at[len(copies)]
+                )
+            )
     for copy in copies:
         copy.start()
     for copy in copies:
@@ -879,6 +914,7 @@
             pltpu.VMEM((batch, LANES), wide),
             pltpu.VMEM((batch, LANES), wide),
             pltpu.VMEM((batch, cells // 2), wide),
+            pltpu.VMEM((batch, batch), narrow),
             pltpu.VMEM((width, cells), narrow),
             pltpu.VMEM((width, cells), narrow),
             pltpu.VMEM(own_hidden.shape, narrow),
@@ -943,7 +979,7 @@
         out_shape=tuple(jax.ShapeDtypeStruct(v.shape, v.dtype) for v in results),
         in_specs=[anywhere] * 3,
         out_specs=[anywhere] * 3,
-        scratch_shapes=[dma((3,))],
+        scratch_shapes=[dma((12,))],
         compiler_params=pltpu.CompilerParams(vmem_limit_bytes=1 << 20),
     )(*results)
 

time: 98.1 us -> 95.1 us (0.969)
  Pallas kernels: 97.2 us -> 94.2 us
    pallas_call x1, Pallas kernels: 94 us -> 91 us  [fused_step(): pl.pallas_call(functools.partial(train_kernel, groups), out_shape=(jax.Sh...]
where the time goes in v6:
time: 95.1 us; the launch traced here: 95 us
  Pallas kernels  94.2 us (99%)
    pallas_call x1, Pallas kernels, fused_step(): pl.pallas_call(functools.partial(train_kernel, groups), out_shape=(jax.Sh...  91 us
    pallas_call x1, Pallas kernels, fused_step(): pl.pallas_call(store_kernel, out_shape=tuple((jax.ShapeDtypeStruct(v.shap...  3.18 us

profile of v6, /device:TPU:0, one launch (start us, length us, event | category | flops | bytes accessed | tf_op | source)
XLA Modules:
  0.0 95.0 jit_solution(13971544880946945605)
XLA Ops:
  0.6 91.0 %shard_map.94 = (f32[512,1024]{1,0:T(8,128)S(1)}, f32[1024,1024]{1,0:T(8,128)S(1)}, f32[5,64,1024]{2,1,0:T(8,128)S(1)}) custom-call(bf16[4,2,2,32,1024]{4,3,2,1,0:T(8,128)(2,1)} %bitcast.16, f32[512,1024]{1,0:T(8,128)} %bitcast.12, f32[1,1024]{1,0:T(1,128)} %bitcast.17, f32[1,1024]{1,0:T(1,128)} %bitcast.18, s32[1,512]{1,0:T(1,128)} %bitcast.19, ...), custom_call_target="tpu_custom_call" | custom-call | flops 32212254720 | bytes 20971520 | tf_op jit(solution)/shard_map/pallas_call | solution.py:899
  91.6 3.2 %shard_map.95 = (f32[512,1024]{1,0:T(8,128)}, f32[1024,1024]{1,0:T(8,128)}, f32[5,64,1024]{2,1,0:T(8,128)}) custom-call(f32[512,1024]{1,0:T(8,128)S(1)} %get-tuple-element.9.refs_0_, f32[1024,1024]{1,0:T(8,128)S(1)} %get-tuple-element.10.refs_1_, f32[5,64,1024]{2,1,0:T(8,128)S(1)} %get-tuple-element.11.refs_2_), custom_call_target="tpu_custom_call" | custom-call | tf_op jit(solution)/shard_map/pallas_call | solution.py:977

commit v7 on v6

--- a/solution.py
+++ b/solution.py
@@ -490,8 +490,10 @@
         factors[i, :, :, :, columns] = factor.reshape(groups, 2, rows, COLUMNS)
         return result
 
-    def forward(i):
+    def forward(i, between=None):
         for j, c in enumerate(parts):
+            if between is not None and j == len(parts) // 2:
+                between()
             if i < last:
                 inputs[i, :, :, :, c] = forward_columns(i, c)
                 continue
@@ -500,11 +502,11 @@
                 tops[j - 1].start()
                 tops[j].start()
 
-    def finish(i):
+    def finish(i, between=None):
         remote(
             twice(lambda: weights.at[i, :, :, 1 - core]), (core_send, 0), (core_recv, i), core_peer
         ).wait_recv()
-        forward(i)
+        forward(i, between)
 
     outer = jnp.logical_not(inner)
     lagging = [last, layer_count]
@@ -567,13 +569,13 @@
         cross(i, 2)
         if i > 0:
             finish(i - 1)
-    finish(last - 1)
-
-    @pl.when(outer)
-    def _():
-        for item, k in held[5:]:
-            relay(item, k)
-
+    def relay_held():
+        @pl.when(outer)
+        def _():
+            for item, k in held[5:]:
+                relay(item, k)
+
+    finish(last - 1, relay_held)
     finish(last)
 
     def update_out(j, decay, rate, other):
@@ -816,16 +818,14 @@
                 preferred_element_type=wide,
             )
         halves[i].start()
-        if i < last - 1:
-            update_hidden(i + 2)
 
     @pl.when(trainer)
     def _():
         for j in range(lent, count):
             add_momentum(j)
 
-    update_hidden(1)
-    update_hidden(0)
+    for i in reversed(range(layer_count)):
+        update_hidden(i)
 
     def gone(view, semaphore, slot):
         remote(twice(view), (semaphore, slot), (x_recv, 0), x_peer).wait_send()

time: 95.1 us -> 94.7 us (level)
  no operation moved by 1% of the time
where the time goes in v7:
time: 94.7 us; the launch traced here: 94.5 us
  Pallas kernels  93.7 us (99%)
    pallas_call x1, Pallas kernels, fused_step(): pl.pallas_call(functools.partial(train_kernel, groups), out_shape=(jax.Sh...  90.5 us
    pallas_call x1, Pallas kernels, fused_step(): pl.pallas_call(store_kernel, out_shape=tuple((jax.ShapeDtypeStruct(v.shap...  3.18 us

profile of v7, /device:TPU:0, one launch (start us, length us, event | category | flops | bytes accessed | tf_op | source)
XLA Modules:
  0.0 94.5 jit_solution(14876493873555278858)
XLA Ops:
  0.6 90.5 %shard_map.94 = (f32[512,1024]{1,0:T(8,128)S(1)}, f32[1024,1024]{1,0:T(8,128)S(1)}, f32[5,64,1024]{2,1,0:T(8,128)S(1)}) custom-call(bf16[4,2,2,32,1024]{4,3,2,1,0:T(8,128)(2,1)} %bitcast.16, f32[512,1024]{1,0:T(8,128)} %bitcast.12, f32[1,1024]{1,0:T(1,128)} %bitcast.17, f32[1,1024]{1,0:T(1,128)} %bitcast.18, s32[1,512]{1,0:T(1,128)} %bitcast.19, ...), custom_call_target="tpu_custom_call" | custom-call | flops 32212254720 | bytes 20971520 | tf_op jit(solution)/shard_map/pallas_call | solution.py:899
  91.2 3.2 %shard_map.95 = (f32[512,1024]{1,0:T(8,128)}, f32[1024,1024]{1,0:T(8,128)}, f32[5,64,1024]{2,1,0:T(8,128)}) custom-call(f32[512,1024]{1,0:T(8,128)S(1)} %get-tuple-element.9.refs_0_, f32[1024,1024]{1,0:T(8,128)S(1)} %get-tuple-element.10.refs_1_, f32[5,64,1024]{2,1,0:T(8,128)S(1)} %get-tuple-element.11.refs_2_), custom_call_target="tpu_custom_call" | custom-call | tf_op jit(solution)/shard_map/pallas_call | solution.py:977

commit v8 on v7

--- a/solution.py
+++ b/solution.py
@@ -687,8 +687,6 @@
                 copy.start()
         update_trainer(0)
         lent_target.wait_send()
-        for j in range(lent):
-            gather(j)
 
     @pl.when(solver)
     def _():
@@ -750,7 +748,7 @@
             if made == len(pieces) - 1:
                 for copy in residuals[1:]:
                     copy.start()
-                for j in range(lent, count):
+                for j in range(count):
                     gather(j)
 
         if 0 <= made < len(pieces):
@@ -866,21 +864,15 @@
 
 def store_kernel(*refs):
     semaphores = refs[-1]
-    copies = []
-    for source, target in zip(refs[:3], refs[3:6]):
+    pairs = list(zip(refs[:3], refs[3:6]))
+    for k, (source, target) in enumerate(pairs):
         length = source.shape[0]
         step = length if length % 4 else length // 4
         for at in range(0, length, step):
             band = pl.ds(at, step)
-            copies.append(
-                pltpu.make_async_copy(
-                    source.at[band], target.at[band], semaphores.at[len(copies)]
-                )
-            )
-    for copy in copies:
-        copy.start()
-    for copy in copies:
-        copy.wait()
+            pltpu.make_async_copy(source.at[band], target.at[band], semaphores.at[k]).start()
+    for k, (source, target) in enumerate(pairs):
+        pltpu.make_async_copy(source, target, semaphores.at[k]).wait()
 
 
 def fused_step(fields, velocity, growth, features, assignment, own_out, own_hidden):
@@ -979,7 +971,7 @@
         out_shape=tuple(jax.ShapeDtypeStruct(v.shape, v.dtype) for v in results),
         in_specs=[anywhere] * 3,
         out_specs=[anywhere] * 3,
-        scratch_shapes=[dma((12,))],
+        scratch_shapes=[dma((3,))],
         compiler_params=pltpu.CompilerParams(vmem_limit_bytes=1 << 20),
     )(*results)
 

time: 94.7 us -> 94.6 us (level)
  no operation moved by 1% of the time
where the time goes in v8:
time: 94.6 us; the launch traced here: 94.4 us
  Pallas kernels  93.6 us (99%)
    pallas_call x1, Pallas kernels, fused_step(): pl.pallas_call(functools.partial(train_kernel, groups), out_shape=(jax.Sh...  90.5 us
    pallas_call x1, Pallas kernels, fused_step(): pl.pallas_call(store_kernel, out_shape=tuple((jax.ShapeDtypeStruct(v.shap...  3.1 us

profile of v8, /device:TPU:0, one launch (start us, length us, event | category | flops | bytes accessed | tf_op | source)
XLA Modules:
  0.0 94.4 jit_solution(7715071909844123032)
XLA Ops:
  0.6 90.5 %shard_map.94 = (f32[512,1024]{1,0:T(8,128)S(1)}, f32[1024,1024]{1,0:T(8,128)S(1)}, f32[5,64,1024]{2,1,0:T(8,128)S(1)}) custom-call(bf16[4,2,2,32,1024]{4,3,2,1,0:T(8,128)(2,1)} %bitcast.16, f32[512,1024]{1,0:T(8,128)} %bitcast.12, f32[1,1024]{1,0:T(1,128)} %bitcast.17, f32[1,1024]{1,0:T(1,128)} %bitcast.18, s32[1,512]{1,0:T(1,128)} %bitcast.19, ...), custom_call_target="tpu_custom_call" | custom-call | flops 32212254720 | bytes 20971520 | tf_op jit(solution)/shard_map/pallas_call | solution.py:891
  91.2 3.1 %shard_map.95 = (f32[512,1024]{1,0:T(8,128)}, f32[1024,1024]{1,0:T(8,128)}, f32[5,64,1024]{2,1,0:T(8,128)}) custom-call(f32[512,1024]{1,0:T(8,128)S(1)} %get-tuple-element.9.refs_0_, f32[1024,1024]{1,0:T(8,128)S(1)} %get-tuple-element.10.refs_1_, f32[5,64,1024]{2,1,0:T(8,128)S(1)} %get-tuple-element.11.refs_2_), custom_call_target="tpu_custom_call" | custom-call | tf_op jit(solution)/shard_map/pallas_call | solution.py:969

commit v9 on v8

--- a/solution.py
+++ b/solution.py
@@ -265,7 +265,7 @@
         lambda: (features_hbm, features_ref),
     ]
     loads = [local(views, local_sem, k) for k, views in enumerate(pairs)]
-    for load in loads:
+    for load in [loads[1], loads[0]] + loads[2:]:
         load.start()
     hidden_load, out_loads, small_loads = loads[0], loads[1 : 1 + len(chunks)], loads[1 + len(chunks) :]
     share_order = [last] + list(range(last))

time: 94.6 us -> 94.6 us (level)
  no operation moved by 1% of the time
where the time goes in v9:
time: 94.6 us; the launch traced here: 94.4 us
  Pallas kernels  93.6 us (99%)
    pallas_call x1, Pallas kernels, fused_step(): pl.pallas_call(functools.partial(train_kernel, groups), out_shape=(jax.Sh...  90.5 us
    pallas_call x1, Pallas kernels, fused_step(): pl.pallas_call(store_kernel, out_shape=tuple((jax.ShapeDtypeStruct(v.shap...  3.1 us

profile of v9, /device:TPU:0, one launch (start us, length us, event | category | flops | bytes accessed | tf_op | source)
XLA Modules:
  0.0 94.4 jit_solution(16114901528001143107)
XLA Ops:
  0.6 90.5 %shard_map.94 = (f32[512,1024]{1,0:T(8,128)S(1)}, f32[1024,1024]{1,0:T(8,128)S(1)}, f32[5,64,1024]{2,1,0:T(8,128)S(1)}) custom-call(bf16[4,2,2,32,1024]{4,3,2,1,0:T(8,128)(2,1)} %bitcast.16, f32[512,1024]{1,0:T(8,128)} %bitcast.12, f32[1,1024]{1,0:T(1,128)} %bitcast.17, f32[1,1024]{1,0:T(1,128)} %bitcast.18, s32[1,512]{1,0:T(1,128)} %bitcast.19, ...), custom_call_target="tpu_custom_call" | custom-call | flops 32212254720 | bytes 20971520 | tf_op jit(solution)/shard_map/pallas_call | solution.py:891
  91.2 3.1 %shard_map.95 = (f32[512,1024]{1,0:T(8,128)}, f32[1024,1024]{1,0:T(8,128)}, f32[5,64,1024]{2,1,0:T(8,128)}) custom-call(f32[512,1024]{1,0:T(8,128)S(1)} %get-tuple-element.9.refs_0_, f32[1024,1024]{1,0:T(8,128)S(1)} %get-tuple-element.10.refs_1_, f32[5,64,1024]{2,1,0:T(8,128)S(1)} %get-tuple-element.11.refs_2_), custom_call_target="tpu_custom_call" | custom-call | tf_op jit(solution)/shard_map/pallas_call | solution.py:969
